TPU v7x, 32 devices: a whole 2x2x4 slice. The times are simulated.
32 devices in a mesh: row: 8 (over z, core), col: 4 (over y, x).
Axes of the slice: x: 2, y: 2, z: 4, core: 2. Of those that a mesh axis runs over, the one named last changes fastest.
Arguments:
- coeffs: bfloat16 [256, 64, 128], P(('row', 'col')), may hold values from -6 to 6
- blocks: bfloat16 [16384, 64, 64], P(('row', 'col')), may hold values from -0.046875 to 0.046875
- blk_rows: int32 [16384], P(('row', 'col')), may hold values from 0 to 255, as said below
- blk_cols: int32 [16384], P(('row', 'col')), may hold values from 0 to 255, as said below
- blk_count: int32 [32], P(('row', 'col')), may hold values from 0 to 512, as said below
Outputs:
- product: float32 [256, 64, 128], P(('row', 'col'))
Inputs may be any that keep to these rules, and one draw needn't show every extreme that they name: `blk_rows`: element e belongs to device e // 8 in row+col order. In the first blk_count slots of a device, I <= J, I belongs to a device of the same row index, and J to a device of the same column index whose row index exceeds that of I's device by 0 to 3; the difference 3 occurs in every draw. Later slots hold elements of the device's own row and column groups and are unused; pairs may repeat. `blk_cols`: see blk_rows. `blk_count`: counts differ widely between devices; some device uses all 512 slots in every draw.
All inputs are finite; a program needn't handle non-finite values.
Results may differ from a plain program's by a relative error of at most 0.0003.
Values may be sent and summed in bfloat16 or wider, within the bound.
No kernel may reach another device: no remote copies, remote signals or barrier semaphores. Data moves between devices by JAX's collectives and lax.ppermute only.
A program may use at most 128 MiB of HBM per device.

v0:
```python
import jax
import jax.numpy as jnp
from jax import lax
from jax.sharding import PartitionSpec as P

REACH = 3


def from_behind(block, axis, distance):
    devices = range(lax.axis_size(axis))
    route = [(i - distance, i) for i in devices if i - distance in devices]
    return lax.ppermute(block, axis, route)


def body(coeffs, blocks, blk_rows, blk_cols, blk_count):
    high_precision = lax.Precision.HIGHEST
    elem_dev, width, sides = coeffs.shape
    slot_total = blocks.shape[0]
    my_row = lax.axis_index("row")
    segment = elem_dev * lax.axis_size("col")
    window = (REACH + 1) * elem_dev
    row_group = lax.all_gather(coeffs, "col", axis=0, tiled=True)
    gathered = coeffs
    spread = 1
    for level in range(REACH.bit_length()):
        arrived = from_behind(gathered, "row", -spread)
        gathered = jnp.concatenate([gathered, arrived], axis=0)
        spread = spread * 2
    active = jnp.arange(slot_total, dtype=jnp.int32) < blk_count[0]
    mirror = active & (blk_rows != blk_cols)
    row_local = jnp.clip(blk_rows - my_row * segment, 0, segment - 1)
    col_local = (blk_cols // segment - my_row) * elem_dev + blk_cols % elem_dev
    col_local = jnp.clip(col_local, 0, window - 1)
    column_entries = gathered[col_local]
    row_contributions = jnp.einsum(
        "gjc,gcx->gjx", blocks, column_entries, preferred_element_type=jnp.float32
    )
    row_contributions = row_contributions.reshape(slot_total, width * sides)
    row_select = (
        (row_local[None, :] == jnp.arange(segment, dtype=jnp.int32)[:, None]) & active[None, :]
    ).astype(jnp.float32)
    row_entries = row_group[row_local]
    column_contributions = jnp.einsum(
        "ihv,ihe->ive", blocks, row_entries, preferred_element_type=jnp.float32
    )
    column_contributions = column_contributions.reshape(slot_total, width * sides)
    col_select = (
        (col_local[None, :] == jnp.arange(window, dtype=jnp.int32)[:, None]) & mirror[None, :]
    ).astype(jnp.float32)
    col_part = jnp.dot(
        col_select,
        column_contributions,
        precision=high_precision,
        preferred_element_type=jnp.float32,
    )
    row_part = jnp.dot(
        row_select, row_contributions, precision=high_precision, preferred_element_type=jnp.float32
    )
    row_sums = lax.psum_scatter(row_part, "col", scatter_dimension=0, tiled=True)
    col_sums = col_part[:elem_dev]
    for offset in range(1, REACH + 1):
        piece = col_part[offset * elem_dev : (offset + 1) * elem_dev]
        col_sums = col_sums + from_behind(piece, "row", offset)
    return (row_sums + col_sums).reshape(elem_dev, width, sides)


def solution(mesh):
    placed = (
        P(("row", "col"), None, None),
        P(("row", "col"), None, None),
        P(("row", "col")),
        P(("row", "col")),
        P(("row", "col")),
    )
    return jax.shard_map(
        body, mesh=mesh, in_specs=placed, out_specs=P(("row", "col"), None, None), check_vma=False
    )
```

profile of v0, /device:TPU:0, one launch (start us, length us, event | category | flops | bytes accessed | tf_op | source)
XLA Modules:
  0.0 199.7 jit_solution(3817646635028299067)
XLA Ops:
  6.5 0.0 copy-start.2
  6.5 0.0 all-reduce.3.cloned.1.call-start
  6.5 1.4 collective-permute-start
  8.0 13.1 %all_gather.3 = bf16[32,64,128]{2,1,0:T(8,128)(2,1)S(1)} all-gather(bf16[8,64,128]{2,1,0:T(8,128)(2,1)} %param.5), channel_id=1, replica_groups=mesh['row'=8,'col'=4] {'col'}, dimensions={0}, use_global_device_ids=true | all-gather | bytes 655360 | tf_op jit(solution)/shard_map/all_gather | solution.py:22
  21.1 0.7 compare_select_fusion
  21.8 15.7 %copy.10 = bf16[512,64,64]{1,2,0:T(8,128)(2,1)} copy(bf16[512,64,64]{0,2,1:T(8,128)(2,1)} %param.6) | data formatting | bytes 8388608 | tf_op args[1]
  37.4 0.0 copy-done.2
  38.1 13.4 %gather_fusion.1 = bf16[512,64,128]{2,1,0:T(8,128)(2,1)} fusion(bf16[32,64,128]{2,1,0:T(8,128)(2,1)S(1)} %all_gather.3, s32[1024]{0:T(1024)S(1)} %pad_clamp_fusion), kind=kCustom, calls=%fused_computation.1 | custom fusion | bytes 16779264 | tf_op jit(solution)/shard_map/gather | solution.py:42
  51.5 0.0 copy-start.1
  51.5 0.0 copy-start
  51.5 13.9 %fusion.28 = f32[512,128,64]{1,2,0:T(8,128)} fusion(bf16[512,64,64]{1,2,0:T(8,128)(2,1)} %copy.10, bf16[512,64,128]{2,1,0:T(8,128)(2,1)} %gather_fusion.1), kind=kOutput, calls=%fused_computation.46 | convolution fusion | flops 536870912 | bytes 29360128 | tf_op jit(solution)/shard_map/ihv,ihe->ive/dot_general | solution.py:43
  65.4 0.0 copy-done.1
  65.4 0.0 collective-permute-done
  65.4 0.0 copy-done
  65.5 1.5 collective-permute-start.1
  66.9 20.3 %fusion = f32[32,8192]{1,0:T(8,128)S(1)} fusion(f32[64,8,64,128]{3,2,1,0:T(8,128)} %bitcast.20, s32[512]{0:T(512)S(1)} %get-tuple-element.6, pred[512]{0:T(512)(128)(4,1)S(1)} %compare_and_fusion), kind=kOutput, calls=%fused_computation.2 | convolution fusion | flops 1610645504 | bytes 17828352 | tf_op jit(solution)/shard_map/dot_general | solution.py:50
  87.3 0.0 collective-permute-done.1
  87.3 0.1 pad_maximum_fusion
  87.4 13.6 %gather_fusion = bf16[512,64,128]{2,1,0:T(8,128)(2,1)} fusion(bf16[32,64,128]{2,1,0:T(8,128)(2,1)S(1)} %pad_maximum_fusion, s32[1024]{0:T(1024)S(1)} %pad_clamp_fusion.1), kind=kCustom, calls=%fused_computation | custom fusion | bytes 16779264 | tf_op jit(solution)/shard_map/gather | solution.py:34
  101.0 14.4 %fusion.27 = f32[512,128,64]{1,2,0:T(8,128)} fusion(bf16[512,64,64]{1,2,0:T(8,128)(2,1)} %copy.10, bf16[512,64,128]{2,1,0:T(8,128)(2,1)} %gather_fusion), kind=kOutput, calls=%fused_computation.45 | convolution fusion | flops 536870912 | bytes 29360128 | tf_op jit(solution)/shard_map/gjc,gcx->gjx/dot_general | solution.py:35
  115.4 0.0 copy-start.3
  115.4 21.2 %fusion.3 = f32[32,8192]{1,0:T(8,128)} fusion(f32[64,8,64,128]{3,2,1,0:T(8,128)} %bitcast.21, s32[512]{0:T(512)S(1)} %get-tuple-element.8, pred[512]{0:T(512)(128)(4,1)S(1)} %iota_compare_fusion.2), kind=kOutput, calls=%fused_computation.5 | convolution fusion | flops 1610645504 | bytes 17828352 | tf_op jit(solution)/shard_map/dot_general | solution.py:56
  136.6 0.0 all-reduce.3.cloned.1.call-update
  136.6 0.1 fusion.26
  136.7 1.6 collective-permute-start.2
  138.3 5.0 %collective-permute-start.3 = (f32[8,8192]{1,0:T(8,128)S(1)}, f32[8,8192]{1,0:T(8,128)S(1)}, u32[]{:S(2)}, u32[]{:S(2)}) collective-permute-start(f32[8,8192]{1,0:T(8,128)S(1)} %get-tuple-element.11), channel_id=1, source_target_pairs={{0,8},{4,12},{8,16},{12,20},{16,24},{20,28},{1,9},{5,13},{9,17},{1... | collective-permute-start | bytes 786440 | tf_op jit(solution)/shard_map/ppermute | solution.py:12
  143.3 4.9 %collective-permute-start.4 = (f32[8,8192]{1,0:T(8,128)S(1)}, f32[8,8192]{1,0:T(8,128)S(1)}, u32[]{:S(2)}, u32[]{:S(2)}) collective-permute-start(f32[8,8192]{1,0:T(8,128)S(1)} %get-tuple-element.10), channel_id=1, source_target_pairs={{0,12},{4,16},{8,20},{12,24},{16,28},{1,13},{5,17},{9,21},{13,25},... | collective-permute-start | bytes 786440 | tf_op jit(solution)/shard_map/ppermute | solution.py:12
  148.2 0.0 copy-done.3
  148.2 0.6 dynamic-slice
  149.5 0.0 collective-permute-done.2
  149.5 0.0 collective-permute-done.3
  149.5 5.5 %collective-permute-done.4 = f32[8,8192]{1,0:T(8,128)S(1)} collective-permute-done((f32[8,8192]{1,0:T(8,128)S(1)}, f32[8,8192]{1,0:T(8,128)S(1)}, u32[]{:S(2)}, u32[]{:S(2)}) %collective-permute-start.4) | collective-permute-done | bytes 262176 | tf_op jit(solution)/shard_map/ppermute | solution.py:12
  155.0 36.1 %all-reduce.3.cloned.1.call-done = f32[32,8192]{1,0:T(8,128)} async-done(((f32[32,8192]{1,0:T(8,128)}), f32[32,8192]{1,0:T(8,128)}) %all-reduce.3.cloned.1.call-update) | async-done | bytes 1048592
  191.1 1.0 fusion.9
  192.1 0.8 copy.11
  (6 shorter events, 0.1 us)
Async XLA Ops:
  6.5 30.9 %copy-start.2 = (s32[512]{0:T(512)S(1)}, s32[512]{0:T(512)}, u32[]{:S(2)}) copy-start(s32[512]{0:T(512)} %param.8) | copy-start | bytes 6148
  6.5 184.6 %all-reduce.3.cloned.1.call-start = ((), (), s32[]{:S(2)}) async-start(), calls=%async_computation | async-start | bytes 2097152
  6.5 58.9 %collective-permute-start = (bf16[8,64,128]{2,1,0:T(8,128)(2,1)}, bf16[8,64,128]{2,1,0:T(8,128)(2,1)S(1)}, u32[]{:S(2)}, u32[]{:S(2)}) collective-permute-start(bf16[8,64,128]{2,1,0:T(8,128)(2,1)} %param.5), channel_id=1, source_target_pairs={{4,0},{8,4},{12,8},{16,12},{20,16},{24,20},{28,24},{5,1},{9,5},{13... | collective-permute-start | bytes 393224 | tf_op jit(solution)/shard_map/ppermute | solution.py:12
  51.5 13.9 %copy-start.1 = (s32[512]{0:T(512)S(1)}, s32[512]{0:T(512)}, u32[]{:S(2)}) copy-start(s32[512]{0:T(512)} %param.7) | copy-start | bytes 6148
  51.5 13.9 %copy-start = (bf16[8,64,128]{2,1,0:T(8,128)(2,1)S(1)}, bf16[8,64,128]{2,1,0:T(8,128)(2,1)}, u32[]{:S(2)}) copy-start(bf16[8,64,128]{2,1,0:T(8,128)(2,1)} %param.5) | copy-start | bytes 393220
  65.5 21.9 %collective-permute-start.1 = (bf16[16,64,128]{2,1,0:T(8,128)(2,1)S(1)}, bf16[16,64,128]{2,1,0:T(8,128)(2,1)S(1)}, u32[]{:S(2)}, u32[]{:S(2)}) collective-permute-start(bf16[16,64,128]{2,1,0:T(8,128)(2,1)S(1)} %pad_maximum_fusion.1), channel_id=1, source_target_pairs={{8,0},{12,4},{16,8},{20,12},{24,16},{28,20},{9,1},{13,5},{17,9},{2... | collective-permute-start | bytes 786440 | tf_op jit(solution)/shard_map/ppermute | solution.py:12
  115.4 32.8 %copy-start.3 = (u32[32]{0:T(128)S(1)}, u32[32]{0:T(128)}, u32[]{:S(2)}) copy-start(u32[32]{0:T(128)} %constant.46) | copy-start | bytes 388
  136.7 12.8 %collective-permute-start.2 = (f32[8,8192]{1,0:T(8,128)S(1)}, f32[8,8192]{1,0:T(8,128)S(1)}, u32[]{:S(2)}, u32[]{:S(2)}) collective-permute-start(f32[8,8192]{1,0:T(8,128)S(1)} %get-tuple-element.9), channel_id=1, source_target_pairs={{0,4},{4,8},{8,12},{12,16},{16,20},{20,24},{24,28},{1,5},{5,9},{9,... | collective-permute-start | bytes 786440 | tf_op jit(solution)/shard_map/ppermute | solution.py:12
  138.3 11.2 %collective-permute-start.3 = (f32[8,8192]{1,0:T(8,128)S(1)}, f32[8,8192]{1,0:T(8,128)S(1)}, u32[]{:S(2)}, u32[]{:S(2)}) collective-permute-start(f32[8,8192]{1,0:T(8,128)S(1)} %get-tuple-element.11), channel_id=1, source_target_pairs={{0,8},{4,12},{8,16},{12,20},{16,24},{20,28},{1,9},{5,13},{9,17},{1... | collective-permute-start | bytes 786440 | tf_op jit(solution)/shard_map/ppermute | solution.py:12
  143.3 11.7 %collective-permute-start.4 = (f32[8,8192]{1,0:T(8,128)S(1)}, f32[8,8192]{1,0:T(8,128)S(1)}, u32[]{:S(2)}, u32[]{:S(2)}) collective-permute-start(f32[8,8192]{1,0:T(8,128)S(1)} %get-tuple-element.10), channel_id=1, source_target_pairs={{0,12},{4,16},{8,20},{12,24},{16,28},{1,13},{5,17},{9,21},{13,25},... | collective-permute-start | bytes 786440 | tf_op jit(solution)/shard_map/ppermute | solution.py:12
Sparse Core Ops, SparseCore 0:
  136.8 54.3 all-reduce.2
where the time goes:
time: 200 us
  matrix products  69.8 us (35%)
  local copies, waits for them, and re-layouts  44.1 us (22%)
  waiting for transfers between devices  41.7 us (21%)
  between operations  14.8 us (7%)
  starting transfers between devices  14.4 us (7%)
  blocking collectives  13.1 us (7%)
    unnamed x2, waiting for transfers between devices  36.1 us
    dot_general x1, matrix products, body(): jnp.dot(row_select, row_contributions, precision=high_precision, preferre...  21.2 us
    dot_general x1, matrix products, body(): jnp.dot(col_select, column_contributions, precision=high_precision, prefe...  20.3 us
    unnamed x10, local copies, waits for them, and re-layouts  16.3 us
    dot_general x1, matrix products, body(): jnp.einsum('gjc,gcx->gjx', blocks, column_entries, preferred_element_type...  14.4 us
    ppermute x5, starting transfers between devices, from_behind(): return lax.ppermute(block, axis, route)  14.4 us
    dot_general x1, matrix products, body(): jnp.einsum('ihv,ihe->ive', blocks, row_entries, preferred_element_type=jn...  13.9 us
    gather x1, local copies, waits for them, and re-layouts, body(): column_entries = gathered[col_local]  13.6 us
  transfers between devices with their start and end apart: 6, of which 2 were waited for; matrix products, arithmetic and copies ran while one was open for 32% of the time, Pallas kernels for 0%

commit v1 on v0

v1 whole, which is shorter than its diff:
```python
import functools

import jax
import jax.numpy as jnp
from jax import lax
from jax.experimental import pallas as pl
from jax.experimental.pallas import tpu as pltpu
from jax.sharding import PartitionSpec as P

REACH = 3
TILE_SLOTS = 128
STEP_SLOTS = 64
TILE_MIB = 24
SUM_MIB = 24
CODE_ROWS = 16
VMEM = pltpu.VMEM
MIB = 1 << 20


def peers(axis):
    n = lax.axis_size(axis)
    if n & (n - 1) == 0:
        return range(1, n), lambda i, k: i ^ k
    return range(1, n), lambda i, k: (n + k - i) % n


def meet(x, axis, k):
    _, partner = peers(axis)
    return lax.ppermute(x, axis, [(i, partner(i, k)) for i in range(lax.axis_size(axis))])


def shift(x, axis, distance):
    devices = range(lax.axis_size(axis))
    return lax.ppermute(x, axis, [(i, i + distance) for i in devices if i + distance in devices])


def tiles_kernel(blocks_ref, tile_ref, flip_ref, narrow_ref, wide_ref, rows_ref, cols_ref, sems, *, width, slots):
    half = width // 2
    wpitch, spitch = width + 1, half + 1
    parts = blocks_ref.shape[1] // slots

    def fetch(part):
        return pltpu.make_async_copy(
            blocks_ref.at[:, pl.ds(part * slots, slots)], narrow_ref.at[part], sems.at[part]
        )

    for part in range(parts):
        fetch(part).start()

    for part in range(parts):
        fetch(part).wait()
        x_ref = narrow_ref.at[part]

        @pl.loop(0, width, unroll=8)
        def _(r):
            wide_ref[pl.ds(r * wpitch, width), :] = x_ref[
                pl.ds(pl.multiple_of(r * width, width), width), :
            ].astype(jnp.float32)

        @pl.loop(0, half, unroll=8)
        def _(q):
            pair = jnp.concatenate(
                [
                    x_ref[pl.ds(pl.multiple_of(q * width, width), width), :],
                    x_ref[pl.ds(pl.multiple_of((q + half) * width, width), width), :],
                ],
                axis=0,
            )
            rows_ref[pl.ds(q, slots, stride=spitch), :] = pair.astype(jnp.float32).T

        @pl.loop(0, half, unroll=8)
        def _(q):
            pair = jnp.concatenate(
                [
                    wide_ref[pl.ds(q, width, stride=wpitch), :],
                    wide_ref[pl.ds(q + half, width, stride=wpitch), :],
                ],
                axis=0,
            )
            cols_ref[pl.ds(q, slots, stride=spitch), :] = pair.T

        @pl.loop(0, slots, unroll=8)
        def _(s):
            at = pl.ds(pl.multiple_of((part * slots + s) * half, half), half)
            tile_ref[at, :] = rows_ref[pl.ds(s * spitch, half), :].astype(tile_ref.dtype)
            flip_ref[at, :] = cols_ref[pl.ds(s * spitch, half), :].astype(flip_ref.dtype)


def make_tiles(blocks):
    total, width, _ = blocks.shape
    slots, half = TILE_SLOTS, width // 2
    flat = blocks.transpose(1, 2, 0).reshape(width * width, total)
    flat = pltpu.with_memory_space_constraint(flat, pltpu.HBM)
    out = pltpu.VMEM((total * half, 2 * width), blocks.dtype)
    return pl.pallas_call(
        functools.partial(tiles_kernel, width=width, slots=slots),
        out_shape=[out, out],
        in_specs=[pl.BlockSpec(memory_space=pl.ANY)],
        out_specs=[pl.BlockSpec(memory_space=VMEM)] * 2,
        scratch_shapes=[
            VMEM((total // slots, width * width, slots), blocks.dtype),
            VMEM((width * (width + 1), slots), jnp.float32),
            VMEM((slots * (half + 1), 2 * width), jnp.float32),
            VMEM((slots * (half + 1), 2 * width), jnp.float32),
            pltpu.SemaphoreType.DMA((total // slots,)),
        ],
        compiler_params=pltpu.CompilerParams(vmem_limit_bytes=TILE_MIB * MIB),
        cost_estimate=pl.CostEstimate(flops=1 << 30, bytes_accessed=24 * MIB, transcendentals=0),
        name="tiles",
    )(flat)


def encode(total):
    elems, width, sides = total.shape
    top = jnp.maximum(jnp.max(jnp.abs(total), axis=1), 1e-30)
    power = jnp.floor(jnp.log2(top)) + 1.0
    codes = total * jnp.exp2(15.0 - power)[:, None, :]
    codes = jnp.clip(jnp.floor(codes + 0.5), -32767.0, 32767.0)
    power = jnp.concatenate([power, jnp.zeros((CODE_ROWS - elems, sides), jnp.float32)], axis=0)
    return codes, power


def products_kernel(count_ref, row_ref, col_ref, land_ref, tile_ref, flip_ref, *refs, reach, near):
    own_ref = refs[0]
    side_refs = refs[1 : 1 + near]
    far_refs = refs[1 + near : 1 + near + reach]
    outs = refs[1 + near + reach :]
    sum_ref = outs[0]
    side_outs = outs[1 : 1 + near]
    far_outs = outs[1 + near : 1 + near + reach]
    wrow_ref, wcol_ref, arow_ref, acol_ref = outs[1 + near + reach :]
    elems, width, sides = own_ref.shape
    half = width // 2
    me = lax.axis_index("col")
    steps, partner = peers("col")
    at_side = [partner(me, k) * elems for k in steps]
    for w_ref in (wrow_ref, wcol_ref):
        w_ref[:, 0:width, sides : 2 * sides] = jnp.zeros_like(w_ref[:, 0:width, sides : 2 * sides])
        w_ref[:, width : 2 * width, 0:sides] = jnp.zeros_like(w_ref[:, 0:width, 0:sides])

    def place(w_ref, at, ref):
        w_ref[pl.ds(at, elems), 0:width, 0:sides] = ref[...]
        w_ref[pl.ds(at, elems), width : 2 * width, sides : 2 * sides] = ref[...]

    place(wcol_ref, 0, own_ref)
    for d, ref in enumerate(far_refs):
        place(wcol_ref, (d + 1) * elems, ref)
    place(wrow_ref, me * elems, own_ref)
    for k, ref in enumerate(side_refs):
        place(wrow_ref, at_side[k], ref)
    arow_ref[...] = jnp.zeros_like(arow_ref)
    acol_ref[...] = jnp.zeros_like(acol_ref)

    @pl.loop(0, (count_ref[0] + STEP_SLOTS - 1) // STEP_SLOTS)
    def _(step):
        first = step * STEP_SLOTS
        for s in range(STEP_SLOTS):
            at = pl.ds(pl.multiple_of((first + s) * half, half), half)
            i, j, land = row_ref[first + s], col_ref[first + s], land_ref[first + s]
            d = jnp.dot(tile_ref[at, :], wcol_ref[j], preferred_element_type=jnp.float32)
            arow_ref[i, 0:half, :] += d[:, 0:sides]
            arow_ref[i, half:width, :] += d[:, sides : 2 * sides]
            d = jnp.dot(flip_ref[at, :], wrow_ref[i], preferred_element_type=jnp.float32)
            acol_ref[land, 0:half, :] += d[:, 0:sides]
            acol_ref[land, half:width, :] += d[:, sides : 2 * sides]

    sum_ref[...] = arow_ref[pl.ds(me * elems, elems)] + acol_ref[0:elems]
    pieces = [(o, acol_ref, (d + 1) * elems) for d, o in enumerate(far_outs)]
    pieces += [(o, arow_ref, at_side[k]) for k, o in enumerate(side_outs)]
    for o, a_ref, at in pieces:
        codes, power = encode(a_ref[pl.ds(at, elems)])
        o[0 : elems * width, :] = codes.reshape(elems * width, sides).astype(jnp.int32).astype(jnp.int16)
        o[elems * width : elems * width + CODE_ROWS, :] = power.astype(jnp.int32).astype(jnp.int16)


def products(count, row, col, land, tiles, flips, own, side, far):
    elems, width, sides = own.shape
    half = width // 2
    near, reach = len(side), len(far)
    group, window = (near + 1) * elems, (reach + 1) * elems
    code = jax.ShapeDtypeStruct((elems * width + CODE_ROWS, sides), jnp.int16)
    scalar, vector = pl.BlockSpec(memory_space=pltpu.SMEM), pl.BlockSpec(memory_space=VMEM)
    n_out = near + reach
    tiles, flips = (pltpu.with_memory_space_constraint(x, VMEM) for x in (tiles, flips))
    return pl.pallas_call(
        functools.partial(products_kernel, reach=reach, near=near),
        out_shape=[jax.ShapeDtypeStruct(own.shape, jnp.float32)] + [code] * n_out,
        in_specs=[scalar] * 4 + [vector] * (3 + n_out),
        out_specs=[vector] * (1 + n_out),
        scratch_shapes=[
            VMEM((group + 1, 2 * width, 2 * sides), own.dtype),
            VMEM((window + 1, 2 * width, 2 * sides), own.dtype),
            VMEM((group + 1, width, sides), jnp.float32),
            VMEM((window + 1, width, sides), jnp.float32),
        ],
        compiler_params=pltpu.CompilerParams(vmem_limit_bytes=SUM_MIB * MIB),
        cost_estimate=pl.CostEstimate(flops=1 << 32, bytes_accessed=24 * MIB, transcendentals=0),
        name="products",
    )(count, row, col, land, tiles, flips, own, *side, *far)


def finish_kernel(*refs):
    own_ref, codes, out_ref = refs[0], refs[1:-1], refs[-1]
    elems, width, sides = own_ref.shape
    total = own_ref[...]
    for ref in codes:
        power = ref[elems * width : elems * width + CODE_ROWS, :].astype(jnp.float32)[0:elems]
        value = ref[0 : elems * width, :].astype(jnp.float32).reshape(elems, width, sides)
        total = total + value * jnp.exp2(power - 15.0)[:, None, :]
    out_ref[...] = total


def finish(own, codes):
    vm = pl.BlockSpec(memory_space=VMEM)
    return pl.pallas_call(
        finish_kernel,
        out_shape=jax.ShapeDtypeStruct(own.shape, jnp.float32),
        in_specs=[vm] * (1 + len(codes)),
        out_specs=vm,
        compiler_params=pltpu.CompilerParams(vmem_limit_bytes=16 * MIB),
        name="finish",
    )(own, *codes)


def body(coeffs, blocks, blk_rows, blk_cols, blk_count):
    elems, width, sides = coeffs.shape
    total = blocks.shape[0]
    my_row = lax.axis_index("row")
    cols = lax.axis_size("col")
    segment, window = elems * cols, (REACH + 1) * elems
    steps, _ = peers("col")
    far = [shift(coeffs, "row", -d) for d in range(1, REACH + 1)]
    side = [meet(coeffs, "col", k) for k in steps]
    tiles, flips = make_tiles(blocks)
    active = jnp.arange(total, dtype=jnp.int32) < blk_count[0]
    row = jnp.clip(blk_rows - my_row * segment, 0, segment - 1)
    row = jnp.where(active, row, segment)
    col = (blk_cols // segment - my_row) * elems + blk_cols % elems
    col = jnp.clip(col, 0, window - 1)
    land = jnp.where(active & (blk_rows != blk_cols), col, window)
    own, *codes = products(blk_count, row, col, land, tiles, flips, coeffs, side, far)
    side_codes, far_codes = codes[: len(side)], codes[len(side) :]
    got = [shift(c, "row", d + 1) for d, c in enumerate(far_codes)]
    got += [meet(c, "col", k) for k, c in zip(steps, side_codes)]
    return finish(own, got)


def solution(mesh):
    placed = (
        P(("row", "col"), None, None),
        P(("row", "col"), None, None),
        P(("row", "col")),
        P(("row", "col")),
        P(("row", "col")),
    )
    return jax.shard_map(
        body, mesh=mesh, in_specs=placed, out_specs=P(("row", "col"), None, None), check_vma=False
    )
```

time: 200 us -> 49.9 us (0.25)
  matrix products: 69.8 us -> 0 us
  local copies, waits for them, and re-layouts: 44.1 us -> 0.01 us
  waiting for transfers between devices: 41.7 us -> 7.03 us
  Pallas kernels: 0 us -> 15.1 us
  between operations: 14.8 us -> 0.78 us
  blocking collectives: 13.1 us -> 0 us
  starting transfers between devices: 14.4 us -> 26.5 us
    dot_general x4 -> x0, matrix products: 69.8 us -> none  [the longest x1 21.2 us: body(): jnp.dot(row_select, row_contributions, precision=high_precision, preferre...]
    unnamed x2 -> x0, waiting for transfers between devices: 36.1 us -> none
    gather x2 -> x0, local copies, waits for them, and re-layouts: 27.1 us -> none  [the longest x1 13.6 us: body(): column_entries = gathered[col_local]]
    unnamed x10 -> x2, local copies, waits for them, and re-layouts: 16.3 us -> 0.01 us
    pallas_call x0 -> x3, Pallas kernels: none -> 15.1 us  [the longest x1 8.54 us: make_tiles(): pl.pallas_call(functools.partial(tiles_kernel, width=width, slots=slots),...]
    all_gather x1 -> x0, blocking collectives: 13.1 us -> none  [body(): row_group = lax.all_gather(coeffs, 'col', axis=0, tiled=True)]
    ppermute x5 -> x12, starting transfers between devices: 14.4 us -> 26.5 us  [the longest x6 18.3 us: shift(): lax.ppermute(x, axis, [(i, i + distance) for i in devices if i + distance...]
    ppermute x5 -> x12, waiting for transfers between devices: 5.54 us -> 7.03 us  [the longest x6 6.24 us: meet(): lax.ppermute(x, axis, [(i, partner(i, k)) for i in range(lax.axis_size(ax...]
  transfers between devices with their start and end apart: 6 -> 12, of which waited for: 2 -> 4; matrix products, arithmetic and copies ran while one was open for 32% -> 1% of each run, Pallas kernels for 0% -> 17%
where the time goes in v1:
time: 49.9 us; the launch traced here: 50.1 us
  starting transfers between devices  26.5 us (53%)
  Pallas kernels  15.1 us (30%)
  waiting for transfers between devices  7.03 us (14%)
  between operations  0.78 us (2%)
  other arithmetic  0.72 us (1%)
    ppermute x6, starting transfers between devices, shift(): lax.ppermute(x, axis, [(i, i + distance) for i in devices if i + distance...  18.3 us
    pallas_call x1, Pallas kernels, make_tiles(): pl.pallas_call(functools.partial(tiles_kernel, width=width, slots=slots),...  8.54 us
    ppermute x6, starting transfers between devices, meet(): lax.ppermute(x, axis, [(i, partner(i, k)) for i in range(lax.axis_size(ax...  8.18 us
    ppermute x6, waiting for transfers between devices, meet(): lax.ppermute(x, axis, [(i, partner(i, k)) for i in range(lax.axis_size(ax...  6.24 us
    pallas_call x1, Pallas kernels, products(): pl.pallas_call(functools.partial(products_kernel, reach=reach, near=near)...  5.63 us
  transfers between devices with their start and end apart: 12, of which 4 were waited for; matrix products, arithmetic and copies ran while one was open for 1% of the time, Pallas kernels for 17%

profile of v1, /device:TPU:0, one launch (start us, length us, event | category | flops | bytes accessed | tf_op | source)
XLA Modules:
  0.0 50.1 jit_solution(5912195459790025727)
XLA Ops:
  0.0 0.0 copy-start
  0.0 1.4 %collective-permute-start.4 = (bf16[8,64,128]{2,1,0:T(8,128)(2,1)}, bf16[8,64,128]{2,1,0:T(8,128)(2,1)S(1)}, u32[]{:S(2)}, u32[]{:S(2)}) collective-permute-start(bf16[8,64,128]{2,1,0:T(8,128)(2,1)} %refs_0_.1), channel_id=1, source_target_pairs={{8,0},{12,4},{16,8},{20,12},{24,16},{28,20},{9,1},{13,5},{17,9},{2... | collective-permute-start | bytes 393224 | tf_op jit(solution)/shard_map/ppermute | solution.py:34
  1.4 1.3 %collective-permute-start.3 = (bf16[8,64,128]{2,1,0:T(8,128)(2,1)}, bf16[8,64,128]{2,1,0:T(8,128)(2,1)S(1)}, u32[]{:S(2)}, u32[]{:S(2)}) collective-permute-start(bf16[8,64,128]{2,1,0:T(8,128)(2,1)} %refs_0_.1), channel_id=1, source_target_pairs={{4,0},{8,4},{12,8},{16,12},{20,16},{24,20},{28,24},{5,1},{9,5},{13... | collective-permute-start | bytes 393224 | tf_op jit(solution)/shard_map/ppermute | solution.py:34
  2.7 4.0 %collective-permute-start.2 = (bf16[8,64,128]{2,1,0:T(8,128)(2,1)}, bf16[8,64,128]{2,1,0:T(8,128)(2,1)S(1)}, u32[]{:S(2)}, u32[]{:S(2)}) collective-permute-start(bf16[8,64,128]{2,1,0:T(8,128)(2,1)} %refs_0_.1), channel_id=1, source_target_pairs={{0,3},{1,2},{2,1},{3,0},{4,7},{5,6},{6,5},{7,4},{8,11},{9,10},{10,... | collective-permute-start | bytes 393224 | tf_op jit(solution)/shard_map/ppermute | solution.py:29
  6.7 0.5 %collective-permute-start.1 = (bf16[8,64,128]{2,1,0:T(8,128)(2,1)}, bf16[8,64,128]{2,1,0:T(8,128)(2,1)S(1)}, u32[]{:S(2)}, u32[]{:S(2)}) collective-permute-start(bf16[8,64,128]{2,1,0:T(8,128)(2,1)} %refs_0_.1), channel_id=1, source_target_pairs={{0,2},{1,3},{2,0},{3,1},{4,6},{5,7},{6,4},{7,5},{8,10},{9,11},{10,... | collective-permute-start | bytes 393224 | tf_op jit(solution)/shard_map/ppermute | solution.py:29
  7.2 0.1 collective-permute-start
  8.0 0.8 %collective-permute-done.4.refs_5_ = bf16[8,64,128]{2,1,0:T(8,128)(2,1)S(1)} collective-permute-done((bf16[8,64,128]{2,1,0:T(8,128)(2,1)}, bf16[8,64,128]{2,1,0:T(8,128)(2,1)S(1)}, u32[]{:S(2)}, u32[]{:S(2)}) %collective-permute-start.4) | collective-permute-done | bytes 131104 | tf_op jit(solution)/shard_map/ppermute | solution.py:34
  8.8 1.3 %collective-permute-start.5 = (bf16[8,64,128]{2,1,0:T(8,128)(2,1)}, bf16[8,64,128]{2,1,0:T(8,128)(2,1)S(1)}, u32[]{:S(2)}, u32[]{:S(2)}) collective-permute-start(bf16[8,64,128]{2,1,0:T(8,128)(2,1)} %refs_0_.1), channel_id=1, source_target_pairs={{12,0},{16,4},{20,8},{24,12},{28,16},{13,1},{17,5},{21,9},{25,13},... | collective-permute-start | bytes 393224 | tf_op jit(solution)/shard_map/ppermute | solution.py:34
  10.1 0.7 %fusion.6 = (s32[512]{0:T(512)S(1)}, s32[512]{0:T(512)S(1)}, s32[512]{0:T(512)S(1)}) fusion(s32[512]{0:T(512)} %param.7, s32[512]{0:T(512)} %param.8, s32[]{:T(128)} %bitcast.4, s32[]{:T(128)S(6)} %axis_index.15, s32[]{:T(128)S(6)} %mul.9), kind=kLoop, calls=%fused_computation.15 | loop fusion | flops 17408 | bytes 10252 | tf_op jit(solution)/shard_map/jit(_where)/select_n | solution.py:240
  10.8 8.5 %tiles.1 = (bf16[16384,128]{1,0:T(8,128)(2,1)S(1)}, bf16[16384,128]{1,0:T(8,128)(2,1)S(1)}) custom-call(bf16[4096,512]{1,0:T(8,128)(2,1)} %bitcast.5), custom_call_target="tpu_custom_call" | custom-call | flops 1073741824 | bytes 25165824 | tf_op jit(solution)/shard_map/tiles/pallas_call | solution.py:95
  19.3 0.0 collective-permute-done.3.refs_4_
  19.3 0.0 collective-permute-done.2.refs_3_
  19.4 0.0 collective-permute-done.1.refs_2_
  19.4 0.0 collective-permute-done.refs_1_
  19.4 0.0 collective-permute-done.5.refs_6_
  19.4 0.0 copy-done
  19.4 5.6 %products.1 = (f32[8,64,128]{2,1,0:T(8,128)S(1)}, s16[528,128]{1,0:T(8,128)(2,1)S(1)}, s16[528,128]{1,0:T(8,128)(2,1)S(1)}, s16[528,128]{1,0:T(8,128)(2,1)S(1)},...) custom-call(s32[1]{0:T(128)} %copy.6.count_ref, ...), custom_call_target="tpu_custom_call" | custom-call | flops 4294967296 | bytes 25165824 | tf_op jit(solution)/shard_map/products/pallas_call | solution.py:185
  25.0 1.3 %collective-permute-start.6 = (s16[528,128]{1,0:T(8,128)(2,1)S(1)}, s16[528,128]{1,0:T(8,128)(2,1)S(1)}, u32[]{:S(2)}, u32[]{:S(2)}) collective-permute-start(s16[528,128]{1,0:T(8,128)(2,1)S(1)} %get-tuple-element.17), channel_id=1, source_target_pairs={{0,4},{4,8},{8,12},{12,16},{16,20},{20,24},{24,28},{1,5},{5,9},{9,... | collective-permute-start | bytes 405512 | tf_op jit(solution)/shard_map/ppermute | solution.py:34
  26.3 8.8 %collective-permute-start.7 = (s16[528,128]{1,0:T(8,128)(2,1)S(1)}, s16[528,128]{1,0:T(8,128)(2,1)S(1)}, u32[]{:S(2)}, u32[]{:S(2)}) collective-permute-start(s16[528,128]{1,0:T(8,128)(2,1)S(1)} %get-tuple-element.18), channel_id=1, source_target_pairs={{0,8},{4,12},{8,16},{12,20},{16,24},{20,28},{1,9},{5,13},{9,17},{1... | collective-permute-start | bytes 405512 | tf_op jit(solution)/shard_map/ppermute | solution.py:34
  35.2 4.2 %collective-permute-start.8 = (s16[528,128]{1,0:T(8,128)(2,1)S(1)}, s16[528,128]{1,0:T(8,128)(2,1)S(1)}, u32[]{:S(2)}, u32[]{:S(2)}) collective-permute-start(s16[528,128]{1,0:T(8,128)(2,1)S(1)} %get-tuple-element.19), channel_id=1, source_target_pairs={{0,12},{4,16},{8,20},{12,24},{16,28},{1,13},{5,17},{9,21},{13,25},... | collective-permute-start | bytes 405512 | tf_op jit(solution)/shard_map/ppermute | solution.py:34
  39.4 0.1 collective-permute-start.9
  39.5 2.1 %collective-permute-start.10 = (s16[528,128]{1,0:T(8,128)(2,1)S(1)}, s16[528,128]{1,0:T(8,128)(2,1)S(1)}, u32[]{:S(2)}, u32[]{:S(2)}) collective-permute-start(s16[528,128]{1,0:T(8,128)(2,1)S(1)} %get-tuple-element.21), channel_id=1, source_target_pairs={{0,2},{1,3},{2,0},{3,1},{4,6},{5,7},{6,4},{7,5},{8,10},{9,11},{10,... | collective-permute-start | bytes 405512 | tf_op jit(solution)/shard_map/ppermute | solution.py:29
  41.6 0.0 collective-permute-done.6.refs_1_
  41.6 1.4 %collective-permute-start.11 = (s16[528,128]{1,0:T(8,128)(2,1)S(1)}, s16[528,128]{1,0:T(8,128)(2,1)S(1)}, u32[]{:S(2)}, u32[]{:S(2)}) collective-permute-start(s16[528,128]{1,0:T(8,128)(2,1)S(1)} %get-tuple-element.22), channel_id=1, source_target_pairs={{0,3},{1,2},{2,1},{3,0},{4,7},{5,6},{6,5},{7,4},{8,11},{9,10},{10,... | collective-permute-start | bytes 405512 | tf_op jit(solution)/shard_map/ppermute | solution.py:29
  43.0 0.0 collective-permute-done.7.refs_2_
  43.0 0.0 collective-permute-done.8.refs_3_
  43.0 2.9 %collective-permute-done.9.refs_4_ = s16[528,128]{1,0:T(8,128)(2,1)S(1)} collective-permute-done((s16[528,128]{1,0:T(8,128)(2,1)S(1)}, s16[528,128]{1,0:T(8,128)(2,1)S(1)}, u32[]{:S(2)}, u32[]{:S(2)}) %collective-permute-start.9) | collective-permute-done | bytes 135200 | tf_op jit(solution)/shard_map/ppermute | solution.py:29
  45.9 1.5 %collective-permute-done.10.refs_5_ = s16[528,128]{1,0:T(8,128)(2,1)S(1)} collective-permute-done((s16[528,128]{1,0:T(8,128)(2,1)S(1)}, s16[528,128]{1,0:T(8,128)(2,1)S(1)}, u32[]{:S(2)}, u32[]{:S(2)}) %collective-permute-start.10) | collective-permute-done | bytes 135200 | tf_op jit(solution)/shard_map/ppermute | solution.py:29
  47.4 1.8 %collective-permute-done.11.refs_6_ = s16[528,128]{1,0:T(8,128)(2,1)S(1)} collective-permute-done((s16[528,128]{1,0:T(8,128)(2,1)S(1)}, s16[528,128]{1,0:T(8,128)(2,1)S(1)}, u32[]{:S(2)}, u32[]{:S(2)}) %collective-permute-start.11) | collective-permute-done | bytes 135200 | tf_op jit(solution)/shard_map/ppermute | solution.py:29
  49.2 0.9 %finish.1 = f32[8,64,128]{2,1,0:T(8,128)} custom-call(f32[8,64,128]{2,1,0:T(8,128)S(1)} %get-tuple-element.16.refs_0_, s16[528,128]{1,0:T(8,128)(2,1)S(1)} %collective-permute-done.6.refs_1_, s16[528,128]{1,0:T(8,128)(2,1)S(1)} %collective-permute-done.7.refs_2_, s16[528,128]{1,0:T(8,128)(2,1)S(1)} %collective-permute-done.8.refs_3_, ...), custom_call_target="tpu_custom_call" | custom-call | tf_op jit(solution)/shard_map/finish/pallas_call | solution.py:215
Async XLA Ops:
  0.0 19.4 %copy-start = (bf16[8,64,128]{2,1,0:T(8,128)(2,1)S(1)}, bf16[8,64,128]{2,1,0:T(8,128)(2,1)}, u32[]{:S(2)}) copy-start(bf16[8,64,128]{2,1,0:T(8,128)(2,1)} %refs_0_.1) | copy-start | bytes 393220
  0.0 8.8 %collective-permute-start.4 = (bf16[8,64,128]{2,1,0:T(8,128)(2,1)}, bf16[8,64,128]{2,1,0:T(8,128)(2,1)S(1)}, u32[]{:S(2)}, u32[]{:S(2)}) collective-permute-start(bf16[8,64,128]{2,1,0:T(8,128)(2,1)} %refs_0_.1), channel_id=1, source_target_pairs={{8,0},{12,4},{16,8},{20,12},{24,16},{28,20},{9,1},{13,5},{17,9},{2... | collective-permute-start | bytes 393224 | tf_op jit(solution)/shard_map/ppermute | solution.py:34
  1.4 17.9 %collective-permute-start.3 = (bf16[8,64,128]{2,1,0:T(8,128)(2,1)}, bf16[8,64,128]{2,1,0:T(8,128)(2,1)S(1)}, u32[]{:S(2)}, u32[]{:S(2)}) collective-permute-start(bf16[8,64,128]{2,1,0:T(8,128)(2,1)} %refs_0_.1), channel_id=1, source_target_pairs={{4,0},{8,4},{12,8},{16,12},{20,16},{24,20},{28,24},{5,1},{9,5},{13... | collective-permute-start | bytes 393224 | tf_op jit(solution)/shard_map/ppermute | solution.py:34
  2.7 16.6 %collective-permute-start.2 = (bf16[8,64,128]{2,1,0:T(8,128)(2,1)}, bf16[8,64,128]{2,1,0:T(8,128)(2,1)S(1)}, u32[]{:S(2)}, u32[]{:S(2)}) collective-permute-start(bf16[8,64,128]{2,1,0:T(8,128)(2,1)} %refs_0_.1), channel_id=1, source_target_pairs={{0,3},{1,2},{2,1},{3,0},{4,7},{5,6},{6,5},{7,4},{8,11},{9,10},{10,... | collective-permute-start | bytes 393224 | tf_op jit(solution)/shard_map/ppermute | solution.py:29
  6.7 12.7 %collective-permute-start.1 = (bf16[8,64,128]{2,1,0:T(8,128)(2,1)}, bf16[8,64,128]{2,1,0:T(8,128)(2,1)S(1)}, u32[]{:S(2)}, u32[]{:S(2)}) collective-permute-start(bf16[8,64,128]{2,1,0:T(8,128)(2,1)} %refs_0_.1), channel_id=1, source_target_pairs={{0,2},{1,3},{2,0},{3,1},{4,6},{5,7},{6,4},{7,5},{8,10},{9,11},{10,... | collective-permute-start | bytes 393224 | tf_op jit(solution)/shard_map/ppermute | solution.py:29
  7.2 12.2 %collective-permute-start = (bf16[8,64,128]{2,1,0:T(8,128)(2,1)}, bf16[8,64,128]{2,1,0:T(8,128)(2,1)S(1)}, u32[]{:S(2)}, u32[]{:S(2)}) collective-permute-start(bf16[8,64,128]{2,1,0:T(8,128)(2,1)} %refs_0_.1), channel_id=1, source_target_pairs={{0,1},{1,0},{2,3},{3,2},{4,5},{5,4},{6,7},{7,6},{8,9},{9,8},{10,11... | collective-permute-start | bytes 393224 | tf_op jit(solution)/shard_map/ppermute | solution.py:29
  8.8 10.6 %collective-permute-start.5 = (bf16[8,64,128]{2,1,0:T(8,128)(2,1)}, bf16[8,64,128]{2,1,0:T(8,128)(2,1)S(1)}, u32[]{:S(2)}, u32[]{:S(2)}) collective-permute-start(bf16[8,64,128]{2,1,0:T(8,128)(2,1)} %refs_0_.1), channel_id=1, source_target_pairs={{12,0},{16,4},{20,8},{24,12},{28,16},{13,1},{17,5},{21,9},{25,13},... | collective-permute-start | bytes 393224 | tf_op jit(solution)/shard_map/ppermute | solution.py:34
  25.0 16.6 %collective-permute-start.6 = (s16[528,128]{1,0:T(8,128)(2,1)S(1)}, s16[528,128]{1,0:T(8,128)(2,1)S(1)}, u32[]{:S(2)}, u32[]{:S(2)}) collective-permute-start(s16[528,128]{1,0:T(8,128)(2,1)S(1)} %get-tuple-element.17), channel_id=1, source_target_pairs={{0,4},{4,8},{8,12},{12,16},{16,20},{20,24},{24,28},{1,5},{5,9},{9,... | collective-permute-start | bytes 405512 | tf_op jit(solution)/shard_map/ppermute | solution.py:34
  26.3 16.6 %collective-permute-start.7 = (s16[528,128]{1,0:T(8,128)(2,1)S(1)}, s16[528,128]{1,0:T(8,128)(2,1)S(1)}, u32[]{:S(2)}, u32[]{:S(2)}) collective-permute-start(s16[528,128]{1,0:T(8,128)(2,1)S(1)} %get-tuple-element.18), channel_id=1, source_target_pairs={{0,8},{4,12},{8,16},{12,20},{16,24},{20,28},{1,9},{5,13},{9,17},{1... | collective-permute-start | bytes 405512 | tf_op jit(solution)/shard_map/ppermute | solution.py:34
  35.2 7.8 %collective-permute-start.8 = (s16[528,128]{1,0:T(8,128)(2,1)S(1)}, s16[528,128]{1,0:T(8,128)(2,1)S(1)}, u32[]{:S(2)}, u32[]{:S(2)}) collective-permute-start(s16[528,128]{1,0:T(8,128)(2,1)S(1)} %get-tuple-element.19), channel_id=1, source_target_pairs={{0,12},{4,16},{8,20},{12,24},{16,28},{1,13},{5,17},{9,21},{13,25},... | collective-permute-start | bytes 405512 | tf_op jit(solution)/shard_map/ppermute | solution.py:34
  39.4 6.5 %collective-permute-start.9 = (s16[528,128]{1,0:T(8,128)(2,1)S(1)}, s16[528,128]{1,0:T(8,128)(2,1)S(1)}, u32[]{:S(2)}, u32[]{:S(2)}) collective-permute-start(s16[528,128]{1,0:T(8,128)(2,1)S(1)} %get-tuple-element.20), channel_id=1, source_target_pairs={{0,1},{1,0},{2,3},{3,2},{4,5},{5,4},{6,7},{7,6},{8,9},{9,8},{10,11... | collective-permute-start | bytes 405512 | tf_op jit(solution)/shard_map/ppermute | solution.py:29
  39.5 7.9 %collective-permute-start.10 = (s16[528,128]{1,0:T(8,128)(2,1)S(1)}, s16[528,128]{1,0:T(8,128)(2,1)S(1)}, u32[]{:S(2)}, u32[]{:S(2)}) collective-permute-start(s16[528,128]{1,0:T(8,128)(2,1)S(1)} %get-tuple-element.21), channel_id=1, source_target_pairs={{0,2},{1,3},{2,0},{3,1},{4,6},{5,7},{6,4},{7,5},{8,10},{9,11},{10,... | collective-permute-start | bytes 405512 | tf_op jit(solution)/shard_map/ppermute | solution.py:29
  41.6 7.6 %collective-permute-start.11 = (s16[528,128]{1,0:T(8,128)(2,1)S(1)}, s16[528,128]{1,0:T(8,128)(2,1)S(1)}, u32[]{:S(2)}, u32[]{:S(2)}) collective-permute-start(s16[528,128]{1,0:T(8,128)(2,1)S(1)} %get-tuple-element.22), channel_id=1, source_target_pairs={{0,3},{1,2},{2,1},{3,0},{4,7},{5,6},{6,5},{7,4},{8,11},{9,10},{10,... | collective-permute-start | bytes 405512 | tf_op jit(solution)/shard_map/ppermute | solution.py:29

commit v2 on v1

v2 whole, which is shorter than its diff:
```python
import functools

import jax
import jax.numpy as jnp
from jax import lax
from jax.experimental import pallas as pl
from jax.experimental.pallas import tpu as pltpu
from jax.sharding import PartitionSpec as P

REACH = 3
TILE_SLOTS = 128
STEP_SLOTS = 64
TILE_MIB = 12
SUM_MIB = 8
UNROLL = 8
CODE_ROWS = 16
VMEM = pltpu.VMEM
MIB = 1 << 20


def peers(axis):
    n = lax.axis_size(axis)
    if n & (n - 1) == 0:
        return range(1, n), lambda i, k: i ^ k
    return range(1, n), lambda i, k: (n + k - i) % n


def meet(x, axis, k):
    _, partner = peers(axis)
    return lax.ppermute(x, axis, [(i, partner(i, k)) for i in range(lax.axis_size(axis))])


def shift(x, axis, distance):
    n = lax.axis_size(axis)
    return lax.ppermute(x, axis, [(i, (i + distance) % n) for i in range(n)])


def far_off(x):
    return pltpu.with_memory_space_constraint(x, pltpu.HBM)


def tiles_kernel(
    count_ref, own_hbm, rows_hbm, cols_hbm, blocks_ref, tile_ref, flip_ref, own_ref, row_ref, col_ref, land_ref,
    rows_ref, cols_ref, narrow_ref, wide_ref, sems,
    *, width, slots, elems
):
    half = width // 2
    wpitch, spitch = width + 1, half + 1
    parts = blocks_ref.shape[1] // slots

    def fetch(part):
        return pltpu.make_async_copy(
            blocks_ref.at[:, pl.ds(part * slots, slots)], narrow_ref.at[part], sems.at[part]
        )

    tables = [
        pltpu.make_async_copy(rows_hbm, rows_ref, sems.at[parts]),
        pltpu.make_async_copy(cols_hbm, cols_ref, sems.at[parts + 1]),
    ]
    own_copy = pltpu.make_async_copy(own_hbm, own_ref, sems.at[parts + 2])
    for copy in tables:
        copy.start()
    for part in range(parts):
        fetch(part).start()
    own_copy.start()
    for copy in tables:
        copy.wait()

    segment, window = elems * lax.axis_size("col"), (REACH + 1) * elems
    base = lax.axis_index("row") * segment
    shape = rows_ref.shape
    slot = lax.broadcasted_iota(jnp.int32, shape, 0) * shape[1] + lax.broadcasted_iota(jnp.int32, shape, 1)
    active = slot < count_ref[0]
    rows, cols = rows_ref[...], cols_ref[...]
    ahead = cols - base - lax.axis_index("col") * elems
    col = ahead
    for d in range(1, REACH + 1):
        col = col - jnp.where(ahead >= d * segment, segment - elems, 0)
    col = jnp.clip(col, 0, window - 1)
    row_ref[...] = jnp.where(active, jnp.clip(rows - base, 0, segment - 1), segment)
    col_ref[...] = col
    land_ref[...] = jnp.where(active & (rows != cols), col, window)

    for part in range(parts):
        fetch(part).wait()
        x_ref = narrow_ref.at[part]

        @pl.loop(0, half, unroll=UNROLL)
        def _(q):
            low = x_ref[pl.ds(pl.multiple_of(q * width, width), width), :].astype(jnp.float32)
            high = x_ref[pl.ds(pl.multiple_of((q + half) * width, width), width), :].astype(jnp.float32)
            wide_ref[pl.ds(q * wpitch, width), :] = low
            wide_ref[pl.ds((q + half) * wpitch, width), :] = high
            pair = jnp.concatenate([low, high], axis=0)
            tile_ref[pl.ds(part * slots * spitch + q, slots, stride=spitch), :] = pair.T

        @pl.loop(0, half, unroll=UNROLL)
        def _(q):
            low = wide_ref[pl.ds(q, width, stride=wpitch), :]
            high = wide_ref[pl.ds(q + half, width, stride=wpitch), :]
            pair = jnp.concatenate([low, high], axis=0).astype(x_ref.dtype)
            flip_ref[pl.ds(part * slots * spitch + q, slots, stride=spitch), :] = pair.T.astype(jnp.float32)

    own_copy.wait()


def make_tiles(count, rows, cols, blocks, own):
    total, width, _ = blocks.shape
    slots, half = TILE_SLOTS, width // 2
    flat = far_off(blocks.transpose(1, 2, 0).reshape(width * width, total))
    tiles = VMEM((total * (half + 1), 2 * width), jnp.float32)
    table = jax.ShapeDtypeStruct((total // 128, 128), jnp.int32)
    vector = pl.BlockSpec(memory_space=VMEM)
    tile, flip, own, *tables = pl.pallas_call(
        functools.partial(tiles_kernel, width=width, slots=slots, elems=own.shape[0]),
        out_shape=[tiles] * 2 + [VMEM(own.shape, own.dtype)] + [table] * 3,
        in_specs=[pl.BlockSpec(memory_space=pltpu.SMEM)] + [pl.BlockSpec(memory_space=pl.ANY)] * 4,
        out_specs=[vector] * 6,
        scratch_shapes=[
            VMEM(table.shape, jnp.int32),
            VMEM(table.shape, jnp.int32),
            VMEM((total // slots, width * width, slots), blocks.dtype),
            VMEM((width * (width + 1), slots), jnp.float32),
            pltpu.SemaphoreType.DMA((total // slots + 3,)),
        ],
        compiler_params=pltpu.CompilerParams(vmem_limit_bytes=TILE_MIB * MIB),
        cost_estimate=pl.CostEstimate(flops=1 << 30, bytes_accessed=24 * MIB, transcendentals=0),
        name="tiles",
    )(count, far_off(own), *(far_off(x.reshape(table.shape)) for x in (rows, cols)), flat)
    return tile, flip, own, [t.reshape(total) for t in tables]


def encode(total):
    elems, _, sides = total.shape
    top = jnp.maximum(jnp.max(jnp.abs(total), axis=1), 1e-30)
    power = jnp.floor(jnp.log2(top)) + 1.0
    codes = total * jnp.exp2(15.0 - power)[:, None, :]
    codes = jnp.clip(jnp.floor(codes + 0.5), -32767.0, 32767.0)
    power = jnp.concatenate([power, jnp.zeros((CODE_ROWS - elems, sides), jnp.float32)], axis=0)
    return codes, power


def put_codes(out_ref, total):
    elems, width, sides = total.shape
    codes, power = encode(total)
    out_ref[0 : elems * width, :] = codes.reshape(elems * width, sides).astype(jnp.int32).astype(jnp.int16)
    out_ref[elems * width : elems * width + CODE_ROWS, :] = power.astype(jnp.int32).astype(jnp.int16)


def products_kernel(count_ref, from_ref, to_ref, tile_ref, *refs, to_group, n_in, n_out):
    pieces, refs = refs[:n_in], refs[n_in:]
    more, refs = (refs[:1], refs[1:]) if to_group else ((), refs)
    sum_ref, outs, (x_ref, acc_ref) = refs[0], refs[1:n_out], refs[n_out:]
    elems, width, sides = pieces[0].shape
    half = width // 2
    me = lax.axis_index("col")
    steps, partner = peers("col")
    group = [me * elems] + [partner(me, k) * elems for k in steps]
    window = [d * elems for d in range(REACH + 1)]
    sources, places = (window, group) if to_group else (group, window)
    acc_ref[...] = jnp.zeros_like(acc_ref)
    for at, ref in zip(sources, pieces):
        x_ref[pl.ds(at, elems)] = ref[...]

    @pl.loop(0, (count_ref[0] + STEP_SLOTS - 1) // STEP_SLOTS)
    def _(step):
        first = step * STEP_SLOTS
        zero = jnp.zeros((width, sides), x_ref.dtype)
        for s in range(STEP_SLOTS):
            tile = tile_ref[pl.ds((first + s) * (half + 1), half), :].astype(x_ref.dtype)
            x, to = x_ref[from_ref[first + s]], to_ref[first + s]
            w = jnp.concatenate([jnp.concatenate([x, zero], axis=1), jnp.concatenate([zero, x], axis=1)], axis=0)
            d = jnp.dot(tile, w, preferred_element_type=jnp.float32)
            acc_ref[to, 0:half, :] += d[:, 0:sides]
            acc_ref[to, half:width, :] += d[:, sides : 2 * sides]

    total = acc_ref[pl.ds(places[0], elems)]
    for ref in more:
        total = total + ref[...]
    sum_ref[...] = total
    for at, ref in zip(places[1:], outs):
        put_codes(ref, acc_ref[pl.ds(at, elems)])


def products(count, source, target, tiles, pieces, n_out, more=()):
    elems, width, sides = pieces[0].shape
    n_in, to_group = len(pieces), bool(more)
    code = jax.ShapeDtypeStruct((elems * width + CODE_ROWS, sides), jnp.int16)
    scalar, vector = pl.BlockSpec(memory_space=pltpu.SMEM), pl.BlockSpec(memory_space=VMEM)
    return pl.pallas_call(
        functools.partial(products_kernel, to_group=to_group, n_in=n_in, n_out=n_out),
        out_shape=[jax.ShapeDtypeStruct((elems, width, sides), jnp.float32)] + [code] * (n_out - 1),
        in_specs=[scalar] * 3 + [vector] * (1 + n_in + len(more)),
        out_specs=[vector] * n_out,
        scratch_shapes=[
            VMEM((n_in * elems + 1, width, sides), pieces[0].dtype),
            VMEM((n_out * elems + 1, width, sides), jnp.float32),
        ],
        compiler_params=pltpu.CompilerParams(vmem_limit_bytes=SUM_MIB * MIB),
        cost_estimate=pl.CostEstimate(flops=1 << 31, bytes_accessed=12 * MIB, transcendentals=0),
        name="row_products" if to_group else "col_products",
    )(count, source, target, pltpu.with_memory_space_constraint(tiles, VMEM), *pieces, *more)


def finish_kernel(*refs):
    own_ref, codes, out_ref = refs[0], refs[1:-1], refs[-1]
    elems, width, sides = own_ref.shape
    total = own_ref[...]
    for ref in codes:
        power = ref[elems * width : elems * width + CODE_ROWS, :].astype(jnp.float32)[0:elems]
        value = ref[0 : elems * width, :].astype(jnp.float32).reshape(elems, width, sides)
        total = total + value * jnp.exp2(power - 15.0)[:, None, :]
    out_ref[...] = total


def finish(own, codes):
    vm = pl.BlockSpec(memory_space=VMEM)
    return pl.pallas_call(
        finish_kernel,
        out_shape=jax.ShapeDtypeStruct(own.shape, jnp.float32),
        in_specs=[vm] * (1 + len(codes)),
        out_specs=vm,
        compiler_params=pltpu.CompilerParams(vmem_limit_bytes=16 * MIB),
        name="finish",
    )(own, *codes)


def body(coeffs, blocks, blk_rows, blk_cols, blk_count):
    steps, _ = peers("col")
    reach = range(1, REACH + 1)
    side = [meet(coeffs, "col", k) for k in steps]
    far = [shift(coeffs, "row", -d) for d in reach]
    tiles, flips, mine, (row, col, land) = make_tiles(blk_count, blk_rows, blk_cols, blocks, coeffs)
    own, *codes = products(blk_count, row, land, flips, [mine] + side, 1 + len(far))
    got = []
    for d, c in zip(reach, codes):
        got.append(shift(c, "row", d))
    own, *codes = products(blk_count, col, row, tiles, [mine] + far, 1 + len(side), [own])
    got += [meet(c, "col", k) for k, c in zip(steps, codes)]
    return finish(own, got)


def solution(mesh):
    placed = (
        P(("row", "col"), None, None),
        P(("row", "col"), None, None),
        P(("row", "col")),
        P(("row", "col")),
        P(("row", "col")),
    )
    return jax.shard_map(
        body, mesh=mesh, in_specs=placed, out_specs=P(("row", "col"), None, None), check_vma=False
    )
```

time: 49.9 us -> 46.2 us (0.926)
  starting transfers between devices: 26.5 us -> 17.4 us
  waiting for transfers between devices: 7.03 us -> 14.9 us
  Pallas kernels: 15.1 us -> 13 us
  other arithmetic: 0.72 us -> 0 us
    ppermute x6, starting transfers between devices: 18.3 us -> 4.15 us  [shift(): return lax.ppermute(x, axis, [(i, (i + distance) % n) for i in range(n)])]
    ppermute x6, waiting for transfers between devices: 0.79 us -> 10.4 us  [shift(): return lax.ppermute(x, axis, [(i, (i + distance) % n) for i in range(n)])]
    ppermute x6, starting transfers between devices: 8.18 us -> 13.2 us  [meet(): lax.ppermute(x, axis, [(i, partner(i, k)) for i in range(lax.axis_size(ax...]
    pallas_call x2 -> x3, Pallas kernels: 14.2 us -> 12 us  [the longest x2 6.23 us: products(): pl.pallas_call(functools.partial(products_kernel, to_group=to_group, n_in...]
    ppermute x6, waiting for transfers between devices: 6.24 us -> 4.48 us  [meet(): lax.ppermute(x, axis, [(i, partner(i, k)) for i in range(lax.axis_size(ax...]
    select_n x1 -> x0, other arithmetic: 0.72 us -> none  [body(): land = jnp.where(active & (blk_rows != blk_cols), col, window)]
  transfers between devices with their start and end apart: 12 -> 12, of which waited for: 4 -> 7; matrix products, arithmetic and copies ran while one was open for 1% -> 0% of each run, Pallas kernels for 17% -> 19%
where the time goes in v2:
time: 46.2 us; the launch traced here: 46 us
  starting transfers between devices  17.4 us (38%)
  waiting for transfers between devices  14.9 us (32%)
  Pallas kernels  13 us (28%)
  between operations  0.73 us (2%)
    ppermute x6, starting transfers between devices, meet(): lax.ppermute(x, axis, [(i, partner(i, k)) for i in range(lax.axis_size(ax...  13.2 us
    ppermute x6, waiting for transfers between devices, shift(): return lax.ppermute(x, axis, [(i, (i + distance) % n) for i in range(n)])  10.4 us
    pallas_call x2, Pallas kernels, products(): pl.pallas_call(functools.partial(products_kernel, to_group=to_group, n_in...  6.23 us
    pallas_call x1, Pallas kernels, make_tiles(): pl.pallas_call(functools.partial(tiles_kernel, width=width, slots=slots,...  5.8 us
    ppermute x6, waiting for transfers between devices, meet(): lax.ppermute(x, axis, [(i, partner(i, k)) for i in range(lax.axis_size(ax...  4.48 us
    ppermute x6, starting transfers between devices, shift(): return lax.ppermute(x, axis, [(i, (i + distance) % n) for i in range(n)])  4.15 us
    pallas_call x1, Pallas kernels, finish(): pl.pallas_call(finish_kernel, out_shape=jax.ShapeDtypeStruct(own.shape, j...  0.94 us
  transfers between devices with their start and end apart: 12, of which 7 were waited for; matrix products, arithmetic and copies ran while one was open for 0% of the time, Pallas kernels for 19%

profile of v2, /device:TPU:0, one launch (start us, length us, event | category | flops | bytes accessed | tf_op | source)
XLA Modules:
  0.0 46.0 jit_solution(2948778766154303280)
XLA Ops:
  0.0 3.0 %collective-permute-start.3 = (bf16[8,64,128]{2,1,0:T(8,128)(2,1)}, bf16[8,64,128]{2,1,0:T(8,128)(2,1)S(1)}, u32[]{:S(2)}, u32[]{:S(2)}) collective-permute-start(bf16[8,64,128]{2,1,0:T(8,128)(2,1)} %own_hbm.1), channel_id=1, source_target_pairs={{0,1},{1,0},{2,3},{3,2},{4,5},{5,4},{6,7},{7,6},{8,9},{9,8},{10,11... | collective-permute-start | bytes 393224 | tf_op jit(solution)/shard_map/ppermute | solution.py:30
  3.0 1.5 %collective-permute-start.4 = (bf16[8,64,128]{2,1,0:T(8,128)(2,1)}, bf16[8,64,128]{2,1,0:T(8,128)(2,1)S(1)}, u32[]{:S(2)}, u32[]{:S(2)}) collective-permute-start(bf16[8,64,128]{2,1,0:T(8,128)(2,1)} %own_hbm.1), channel_id=1, source_target_pairs={{0,2},{1,3},{2,0},{3,1},{4,6},{5,7},{6,4},{7,5},{8,10},{9,11},{10,... | collective-permute-start | bytes 393224 | tf_op jit(solution)/shard_map/ppermute | solution.py:30
  4.5 0.0 collective-permute-start.5
  4.5 2.7 %collective-permute-start = (bf16[8,64,128]{2,1,0:T(8,128)(2,1)}, bf16[8,64,128]{2,1,0:T(8,128)(2,1)S(1)}, u32[]{:S(2)}, u32[]{:S(2)}) collective-permute-start(bf16[8,64,128]{2,1,0:T(8,128)(2,1)} %own_hbm.1), channel_id=1, source_target_pairs={{0,28},{4,0},{8,4},{12,8},{16,12},{20,16},{24,20},{28,24},{1,29},{... | collective-permute-start | bytes 393224 | tf_op jit(solution)/shard_map/ppermute | solution.py:35
  7.2 1.4 %collective-permute-start.1 = (bf16[8,64,128]{2,1,0:T(8,128)(2,1)}, bf16[8,64,128]{2,1,0:T(8,128)(2,1)S(1)}, u32[]{:S(2)}, u32[]{:S(2)}) collective-permute-start(bf16[8,64,128]{2,1,0:T(8,128)(2,1)} %own_hbm.1), channel_id=1, source_target_pairs={{0,24},{4,28},{8,0},{12,4},{16,8},{20,12},{24,16},{28,20},{1,25},{... | collective-permute-start | bytes 393224 | tf_op jit(solution)/shard_map/ppermute | solution.py:35
  9.2 5.8 %tiles.1 = (f32[16896,128]{1,0:T(8,128)S(1)}, f32[16896,128]{1,0:T(8,128)S(1)}, bf16[8,64,128]{2,1,0:T(8,128)(2,1)S(1)}, s32[4,128]{1,0:T(4,128)S(1)}, s32[4,128]{1,0:T(4,128)S(1)}, /*index=5*/s32[4,128]{1,0:T(4,128)S(1)}) custom-call(s32[1]{0:T(128)S(6)} %copy.6.count_ref, bf16[8,64,128]{2,1,0:T(8,128)(2,1)} %own_hbm.1, s32[4,128]{1,0:T(4,128)} %bitcast.13, ...), custom_call_target="tpu_custom_call" | custom-call | flops 1073741824 | bytes 25165824 | tf_op jit(solution)/shard_map/tiles/pallas_call | solution.py:114
  15.0 0.0 collective-permute-done.3.refs_1_
  15.0 0.1 collective-permute-start.2
  15.1 0.0 collective-permute-done.4.refs_2_
  15.1 0.0 collective-permute-done.5.refs_3_
  15.1 3.1 %col_products.1 = (f32[8,64,128]{2,1,0:T(8,128)S(1)}, s16[528,128]{1,0:T(8,128)(2,1)S(1)}, s16[528,128]{1,0:T(8,128)(2,1)S(1)}, s16[528,128]{1,0:T(8,128)(2,1)S(1)}) custom-call(s32[1]{0:T(128)S(6)} %copy.6.count_ref, s32[512]{0:T(512)S(1)} %bitcast.8, s32[512]{0:T(512)S(1)} %bitcast.11, f32[16896,128]{1,0:T(8,128)S(1)} %get-tuple-element.24.tile_ref, ...), custom_call_target="tpu_custom_call" | custom-call | flops 2147483648 | bytes 12582912 | tf_op jit(solution)/shard_map/col_products/pallas_call | solution.py:190
  18.3 0.0 collective-permute-done.refs_1_
  18.3 0.0 collective-permute-done.1.refs_2_
  18.3 1.4 %collective-permute-done.2.refs_3_ = bf16[8,64,128]{2,1,0:T(8,128)(2,1)S(1)} collective-permute-done((bf16[8,64,128]{2,1,0:T(8,128)(2,1)}, bf16[8,64,128]{2,1,0:T(8,128)(2,1)S(1)}, u32[]{:S(2)}, u32[]{:S(2)}) %collective-permute-start.2) | collective-permute-done | bytes 131104 | tf_op jit(solution)/shard_map/ppermute | solution.py:35
  19.7 3.1 %row_products.1 = (f32[8,64,128]{2,1,0:T(8,128)S(1)}, s16[528,128]{1,0:T(8,128)(2,1)S(1)}, s16[528,128]{1,0:T(8,128)(2,1)S(1)}, s16[528,128]{1,0:T(8,128)(2,1)S(1)}) custom-call(s32[1]{0:T(128)S(6)} %copy.6.count_ref, s32[512]{0:T(512)S(1)} %bitcast.10, s32[512]{0:T(512)S(1)} %bitcast.9, f32[16896,128]{1,0:T(8,128)S(1)} %get-tuple-element.21.tile_ref, ...), custom_call_target="tpu_custom_call" | custom-call | flops 2147483648 | bytes 12582912 | tf_op jit(solution)/shard_map/row_products/pallas_call | solution.py:190
  22.8 7.2 %collective-permute-start.10 = (s16[528,128]{1,0:T(8,128)(2,1)S(1)}, s16[528,128]{1,0:T(8,128)(2,1)S(1)}, u32[]{:S(2)}, u32[]{:S(2)}) collective-permute-start(s16[528,128]{1,0:T(8,128)(2,1)S(1)} %get-tuple-element.31), channel_id=1, source_target_pairs={{0,2},{1,3},{2,0},{3,1},{4,6},{5,7},{6,4},{7,5},{8,10},{9,11},{10,... | collective-permute-start | bytes 405512 | tf_op jit(solution)/shard_map/ppermute | solution.py:30
  30.0 0.0 collective-permute-start.11
  30.0 1.5 %collective-permute-start.9 = (s16[528,128]{1,0:T(8,128)(2,1)S(1)}, s16[528,128]{1,0:T(8,128)(2,1)S(1)}, u32[]{:S(2)}, u32[]{:S(2)}) collective-permute-start(s16[528,128]{1,0:T(8,128)(2,1)S(1)} %get-tuple-element.30), channel_id=1, source_target_pairs={{0,1},{1,0},{2,3},{3,2},{4,5},{5,4},{6,7},{7,6},{8,9},{9,8},{10,11... | collective-permute-start | bytes 405512 | tf_op jit(solution)/shard_map/ppermute | solution.py:30
  31.6 0.0 collective-permute-start.6
  31.6 0.0 collective-permute-start.7
  31.6 2.5 %collective-permute-done.10.refs_5_ = s16[528,128]{1,0:T(8,128)(2,1)S(1)} collective-permute-done((s16[528,128]{1,0:T(8,128)(2,1)S(1)}, s16[528,128]{1,0:T(8,128)(2,1)S(1)}, u32[]{:S(2)}, u32[]{:S(2)}) %collective-permute-start.10) | collective-permute-done | bytes 135200 | tf_op jit(solution)/shard_map/ppermute | solution.py:30
  34.0 0.0 collective-permute-start.8
  34.0 1.9 %collective-permute-done.11.refs_6_ = s16[528,128]{1,0:T(8,128)(2,1)S(1)} collective-permute-done((s16[528,128]{1,0:T(8,128)(2,1)S(1)}, s16[528,128]{1,0:T(8,128)(2,1)S(1)}, u32[]{:S(2)}, u32[]{:S(2)}) %collective-permute-start.11) | collective-permute-done | bytes 135200 | tf_op jit(solution)/shard_map/ppermute | solution.py:30
  35.9 0.1 collective-permute-done.9.refs_4_
  36.0 2.7 %collective-permute-done.6.refs_1_ = s16[528,128]{1,0:T(8,128)(2,1)S(1)} collective-permute-done((s16[528,128]{1,0:T(8,128)(2,1)S(1)}, s16[528,128]{1,0:T(8,128)(2,1)S(1)}, u32[]{:S(2)}, u32[]{:S(2)}) %collective-permute-start.6) | collective-permute-done | bytes 135200 | tf_op jit(solution)/shard_map/ppermute | solution.py:35
  38.7 1.2 %collective-permute-done.7.refs_2_ = s16[528,128]{1,0:T(8,128)(2,1)S(1)} collective-permute-done((s16[528,128]{1,0:T(8,128)(2,1)S(1)}, s16[528,128]{1,0:T(8,128)(2,1)S(1)}, u32[]{:S(2)}, u32[]{:S(2)}) %collective-permute-start.7) | collective-permute-done | bytes 135200 | tf_op jit(solution)/shard_map/ppermute | solution.py:35
  39.9 5.1 %collective-permute-done.8.refs_3_ = s16[528,128]{1,0:T(8,128)(2,1)S(1)} collective-permute-done((s16[528,128]{1,0:T(8,128)(2,1)S(1)}, s16[528,128]{1,0:T(8,128)(2,1)S(1)}, u32[]{:S(2)}, u32[]{:S(2)}) %collective-permute-start.8) | collective-permute-done | bytes 135200 | tf_op jit(solution)/shard_map/ppermute | solution.py:35
  45.0 0.9 %finish.1 = f32[8,64,128]{2,1,0:T(8,128)} custom-call(f32[8,64,128]{2,1,0:T(8,128)S(1)} %get-tuple-element.26.refs_0_, s16[528,128]{1,0:T(8,128)(2,1)S(1)} %collective-permute-done.6.refs_1_, s16[528,128]{1,0:T(8,128)(2,1)S(1)} %collective-permute-done.7.refs_2_, s16[528,128]{1,0:T(8,128)(2,1)S(1)} %collective-permute-done.8.refs_3_, ...), custom_call_target="tpu_custom_call" | custom-call | tf_op jit(solution)/shard_map/finish/pallas_call | solution.py:218
Async XLA Ops:
  0.0 15.0 %collective-permute-start.3 = (bf16[8,64,128]{2,1,0:T(8,128)(2,1)}, bf16[8,64,128]{2,1,0:T(8,128)(2,1)S(1)}, u32[]{:S(2)}, u32[]{:S(2)}) collective-permute-start(bf16[8,64,128]{2,1,0:T(8,128)(2,1)} %own_hbm.1), channel_id=1, source_target_pairs={{0,1},{1,0},{2,3},{3,2},{4,5},{5,4},{6,7},{7,6},{8,9},{9,8},{10,11... | collective-permute-start | bytes 393224 | tf_op jit(solution)/shard_map/ppermute | solution.py:30
  3.0 12.1 %collective-permute-start.4 = (bf16[8,64,128]{2,1,0:T(8,128)(2,1)}, bf16[8,64,128]{2,1,0:T(8,128)(2,1)S(1)}, u32[]{:S(2)}, u32[]{:S(2)}) collective-permute-start(bf16[8,64,128]{2,1,0:T(8,128)(2,1)} %own_hbm.1), channel_id=1, source_target_pairs={{0,2},{1,3},{2,0},{3,1},{4,6},{5,7},{6,4},{7,5},{8,10},{9,11},{10,... | collective-permute-start | bytes 393224 | tf_op jit(solution)/shard_map/ppermute | solution.py:30
  4.5 10.6 %collective-permute-start.5 = (bf16[8,64,128]{2,1,0:T(8,128)(2,1)}, bf16[8,64,128]{2,1,0:T(8,128)(2,1)S(1)}, u32[]{:S(2)}, u32[]{:S(2)}) collective-permute-start(bf16[8,64,128]{2,1,0:T(8,128)(2,1)} %own_hbm.1), channel_id=1, source_target_pairs={{0,3},{1,2},{2,1},{3,0},{4,7},{5,6},{6,5},{7,4},{8,11},{9,10},{10,... | collective-permute-start | bytes 393224 | tf_op jit(solution)/shard_map/ppermute | solution.py:30
  4.5 13.8 %collective-permute-start = (bf16[8,64,128]{2,1,0:T(8,128)(2,1)}, bf16[8,64,128]{2,1,0:T(8,128)(2,1)S(1)}, u32[]{:S(2)}, u32[]{:S(2)}) collective-permute-start(bf16[8,64,128]{2,1,0:T(8,128)(2,1)} %own_hbm.1), channel_id=1, source_target_pairs={{0,28},{4,0},{8,4},{12,8},{16,12},{20,16},{24,20},{28,24},{1,29},{... | collective-permute-start | bytes 393224 | tf_op jit(solution)/shard_map/ppermute | solution.py:35
  7.2 11.1 %collective-permute-start.1 = (bf16[8,64,128]{2,1,0:T(8,128)(2,1)}, bf16[8,64,128]{2,1,0:T(8,128)(2,1)S(1)}, u32[]{:S(2)}, u32[]{:S(2)}) collective-permute-start(bf16[8,64,128]{2,1,0:T(8,128)(2,1)} %own_hbm.1), channel_id=1, source_target_pairs={{0,24},{4,28},{8,0},{12,4},{16,8},{20,12},{24,16},{28,20},{1,25},{... | collective-permute-start | bytes 393224 | tf_op jit(solution)/shard_map/ppermute | solution.py:35
  15.0 4.7 %collective-permute-start.2 = (bf16[8,64,128]{2,1,0:T(8,128)(2,1)}, bf16[8,64,128]{2,1,0:T(8,128)(2,1)S(1)}, u32[]{:S(2)}, u32[]{:S(2)}) collective-permute-start(bf16[8,64,128]{2,1,0:T(8,128)(2,1)} %own_hbm.1), channel_id=1, source_target_pairs={{0,20},{4,24},{8,28},{12,0},{16,4},{20,8},{24,12},{28,16},{1,21},{... | collective-permute-start | bytes 393224 | tf_op jit(solution)/shard_map/ppermute | solution.py:35
  22.8 11.2 %collective-permute-start.10 = (s16[528,128]{1,0:T(8,128)(2,1)S(1)}, s16[528,128]{1,0:T(8,128)(2,1)S(1)}, u32[]{:S(2)}, u32[]{:S(2)}) collective-permute-start(s16[528,128]{1,0:T(8,128)(2,1)S(1)} %get-tuple-element.31), channel_id=1, source_target_pairs={{0,2},{1,3},{2,0},{3,1},{4,6},{5,7},{6,4},{7,5},{8,10},{9,11},{10,... | collective-permute-start | bytes 405512 | tf_op jit(solution)/shard_map/ppermute | solution.py:30
  30.0 5.9 %collective-permute-start.11 = (s16[528,128]{1,0:T(8,128)(2,1)S(1)}, s16[528,128]{1,0:T(8,128)(2,1)S(1)}, u32[]{:S(2)}, u32[]{:S(2)}) collective-permute-start(s16[528,128]{1,0:T(8,128)(2,1)S(1)} %get-tuple-element.32), channel_id=1, source_target_pairs={{0,3},{1,2},{2,1},{3,0},{4,7},{5,6},{6,5},{7,4},{8,11},{9,10},{10,... | collective-permute-start | bytes 405512 | tf_op jit(solution)/shard_map/ppermute | solution.py:30
  30.0 6.0 %collective-permute-start.9 = (s16[528,128]{1,0:T(8,128)(2,1)S(1)}, s16[528,128]{1,0:T(8,128)(2,1)S(1)}, u32[]{:S(2)}, u32[]{:S(2)}) collective-permute-start(s16[528,128]{1,0:T(8,128)(2,1)S(1)} %get-tuple-element.30), channel_id=1, source_target_pairs={{0,1},{1,0},{2,3},{3,2},{4,5},{5,4},{6,7},{7,6},{8,9},{9,8},{10,11... | collective-permute-start | bytes 405512 | tf_op jit(solution)/shard_map/ppermute | solution.py:30
  31.6 7.2 %collective-permute-start.6 = (s16[528,128]{1,0:T(8,128)(2,1)S(1)}, s16[528,128]{1,0:T(8,128)(2,1)S(1)}, u32[]{:S(2)}, u32[]{:S(2)}) collective-permute-start(s16[528,128]{1,0:T(8,128)(2,1)S(1)} %get-tuple-element.27), channel_id=1, source_target_pairs={{0,4},{4,8},{8,12},{12,16},{16,20},{20,24},{24,28},{28,0},{1,5},{5... | collective-permute-start | bytes 405512 | tf_op jit(solution)/shard_map/ppermute | solution.py:35
  31.6 8.4 %collective-permute-start.7 = (s16[528,128]{1,0:T(8,128)(2,1)S(1)}, s16[528,128]{1,0:T(8,128)(2,1)S(1)}, u32[]{:S(2)}, u32[]{:S(2)}) collective-permute-start(s16[528,128]{1,0:T(8,128)(2,1)S(1)} %get-tuple-element.28), channel_id=1, source_target_pairs={{0,8},{4,12},{8,16},{12,20},{16,24},{20,28},{24,0},{28,4},{1,9},{5... | collective-permute-start | bytes 405512 | tf_op jit(solution)/shard_map/ppermute | solution.py:35
  34.0 11.0 %collective-permute-start.8 = (s16[528,128]{1,0:T(8,128)(2,1)S(1)}, s16[528,128]{1,0:T(8,128)(2,1)S(1)}, u32[]{:S(2)}, u32[]{:S(2)}) collective-permute-start(s16[528,128]{1,0:T(8,128)(2,1)S(1)} %get-tuple-element.29), channel_id=1, source_target_pairs={{0,12},{4,16},{8,20},{12,24},{16,28},{20,0},{24,4},{28,8},{1,13},{... | collective-permute-start | bytes 405512 | tf_op jit(solution)/shard_map/ppermute | solution.py:35

commit v3 on v2

--- a/solution.py
+++ b/solution.py
@@ -9,9 +9,12 @@
 
 REACH = 3
 TILE_SLOTS = 128
-STEP_SLOTS = 64
+STEP_SLOTS = 128
+SHARE = 4
+CHAINS = 2
+LANES = 128
 TILE_MIB = 12
-SUM_MIB = 8
+SUM_MIB = 12
 UNROLL = 8
 CODE_ROWS = 16
 VMEM = pltpu.VMEM
@@ -39,11 +42,61 @@
     return pltpu.with_memory_space_constraint(x, pltpu.HBM)
 
 
+def places_for(total, keys):
+    return -(-(total + keys * (SHARE - 1)) // LANES) * LANES
+
+
+def order_slots(keys, active, dest, n_keys, nowhere, pitch, slot_ref, key_ref, dest_ref, steps_ref):
+    blocks = keys.shape[0]
+    places = slot_ref.shape[0] * LANES
+    keys = jnp.where(active, keys, -1)
+    lane = functools.partial(lax.broadcasted_iota, jnp.int32)
+    which = lane((n_keys, LANES), 0)
+    hits = [(jnp.broadcast_to(keys[b : b + 1], which.shape) == which).astype(jnp.float32) for b in range(blocks)]
+    before = lane((LANES, 2 * LANES), 0) < lane((LANES, 2 * LANES), 1)
+    before = before | (lane((LANES, 2 * LANES), 1) >= LANES)
+    counts = jnp.dot(
+        jnp.concatenate(hits, axis=0).astype(jnp.bfloat16),
+        before.astype(jnp.float32).astype(jnp.bfloat16),
+        preferred_element_type=jnp.float32,
+    )
+    seen, ranks = jnp.zeros((n_keys, LANES), jnp.float32), []
+    for b in range(blocks):
+        at = slice(b * n_keys, (b + 1) * n_keys)
+        ranks.append(counts[at, 0:LANES] + seen)
+        seen = seen + counts[at, LANES : 2 * LANES]
+    chunks = jnp.floor((seen + (SHARE - 1)) * (1.0 / SHARE))
+    lower = (lane((n_keys, n_keys), 1) < lane((n_keys, n_keys), 0)).astype(jnp.float32).astype(jnp.bfloat16)
+    first = SHARE * jnp.dot(lower, chunks.astype(jnp.bfloat16), preferred_element_type=jnp.float32)
+    place = [jnp.sum(h * (r + first + 1.0), axis=0, keepdims=True) - 1.0 for h, r in zip(hits, ranks)]
+    turned = jnp.concatenate(place + [jnp.zeros((LANES - blocks, LANES), jnp.float32)], axis=0).T
+    spread = lane((LANES, places), 1).astype(jnp.float32)
+    found = jnp.zeros((8, places), jnp.float32)
+    for b in range(blocks):
+        chosen = (turned[:, b : b + 1] == spread).astype(jnp.float32).astype(jnp.bfloat16)
+        row = lane((8, LANES), 0)
+        value = jnp.where(row == 0, lane((8, LANES), 1), jnp.where(row == 1, b, 1))
+        value = jnp.where(row == 2, jnp.broadcast_to(dest[b : b + 1], value.shape), value)
+        value = jnp.where(row == 3, jnp.broadcast_to(keys[b : b + 1], value.shape), value)
+        value = value.astype(jnp.float32).astype(jnp.bfloat16)
+        found = found + jnp.dot(value, chosen, preferred_element_type=jnp.float32)
+    found = found.astype(jnp.int32)
+    slot = (found[0:1] + LANES * found[1:2]) * pitch
+    to = jnp.where(found[4:5] > 0, found[2:3], nowhere)
+    for i in range(places // LANES):
+        at = slice(i * LANES, (i + 1) * LANES)
+        slot_ref[i : i + 1, :] = slot[:, at]
+        key_ref[i : i + 1, :] = found[3:4, at]
+        dest_ref[i : i + 1, :] = to[:, at]
+    used = jnp.sum(chunks, axis=0, keepdims=True) * SHARE
+    steps_ref[...] = jnp.floor((used + (STEP_SLOTS - 1)) * (1.0 / STEP_SLOTS)).astype(jnp.int32)
+
+
 def tiles_kernel(
-    count_ref, own_hbm, rows_hbm, cols_hbm, blocks_ref, tile_ref, flip_ref, own_ref, row_ref, col_ref, land_ref,
-    rows_ref, cols_ref, narrow_ref, wide_ref, sems,
-    *, width, slots, elems
+    count_ref, own_hbm, rows_hbm, cols_hbm, blocks_ref, tile_ref, flip_ref, own_ref, *refs,
+    width, slots, elems
 ):
+    group_order, window_order, (rows_ref, cols_ref, narrow_ref, wide_ref, sems) = refs[:4], refs[4:8], refs[8:]
     half = width // 2
     wpitch, spitch = width + 1, half + 1
     parts = blocks_ref.shape[1] // slots
@@ -77,9 +130,9 @@
     for d in range(1, REACH + 1):
         col = col - jnp.where(ahead >= d * segment, segment - elems, 0)
     col = jnp.clip(col, 0, window - 1)
-    row_ref[...] = jnp.where(active, jnp.clip(rows - base, 0, segment - 1), segment)
-    col_ref[...] = col
-    land_ref[...] = jnp.where(active & (rows != cols), col, window)
+    row = jnp.clip(rows - base, 0, segment - 1)
+    order_slots(row, active & (rows != cols), col, segment, window, spitch, *group_order)
+    order_slots(col, active, row, window, segment, spitch, *window_order)
 
     for part in range(parts):
         fetch(part).wait()
@@ -104,18 +157,23 @@
     own_copy.wait()
 
 
-def make_tiles(count, rows, cols, blocks, own):
+def make_tiles(count, rows, columns, blocks, own):
     total, width, _ = blocks.shape
     slots, half = TILE_SLOTS, width // 2
     flat = far_off(blocks.transpose(1, 2, 0).reshape(width * width, total))
     tiles = VMEM((total * (half + 1), 2 * width), jnp.float32)
-    table = jax.ShapeDtypeStruct((total // 128, 128), jnp.int32)
+    table = jax.ShapeDtypeStruct((total // LANES, LANES), jnp.int32)
+    elems, cols = own.shape[0], lax.axis_size("col")
+    orders = []
+    for keys in (elems * cols, elems * (REACH + 1)):
+        orders += [jax.ShapeDtypeStruct((places_for(total, keys) // LANES, LANES), jnp.int32)] * 3
+        orders += [jax.ShapeDtypeStruct((1, LANES), jnp.int32)]
     vector = pl.BlockSpec(memory_space=VMEM)
-    tile, flip, own, *tables = pl.pallas_call(
+    tile, flip, own, *orders = pl.pallas_call(
         functools.partial(tiles_kernel, width=width, slots=slots, elems=own.shape[0]),
-        out_shape=[tiles] * 2 + [VMEM(own.shape, own.dtype)] + [table] * 3,
+        out_shape=[tiles] * 2 + [VMEM(own.shape, own.dtype)] + orders,
         in_specs=[pl.BlockSpec(memory_space=pltpu.SMEM)] + [pl.BlockSpec(memory_space=pl.ANY)] * 4,
-        out_specs=[vector] * 6,
+        out_specs=[vector] * (3 + len(orders)),
         scratch_shapes=[
             VMEM(table.shape, jnp.int32),
             VMEM(table.shape, jnp.int32),
@@ -126,8 +184,8 @@
         compiler_params=pltpu.CompilerParams(vmem_limit_bytes=TILE_MIB * MIB),
         cost_estimate=pl.CostEstimate(flops=1 << 30, bytes_accessed=24 * MIB, transcendentals=0),
         name="tiles",
-    )(count, far_off(own), *(far_off(x.reshape(table.shape)) for x in (rows, cols)), flat)
-    return tile, flip, own, [t.reshape(total) for t in tables]
+    )(count, far_off(own), *(far_off(x.reshape(table.shape)) for x in (rows, columns)), flat)
+    return tile, flip, own, orders[:4], orders[4:]
 
 
 def encode(total):
@@ -147,10 +205,10 @@
     out_ref[elems * width : elems * width + CODE_ROWS, :] = power.astype(jnp.int32).astype(jnp.int16)
 
 
-def products_kernel(count_ref, from_ref, to_ref, tile_ref, *refs, to_group, n_in, n_out):
+def products_kernel(slot_ref, key_ref, to_ref, steps_ref, tile_ref, *refs, to_group, n_in, n_out):
     pieces, refs = refs[:n_in], refs[n_in:]
     more, refs = (refs[:1], refs[1:]) if to_group else ((), refs)
-    sum_ref, outs, (x_ref, acc_ref) = refs[0], refs[1:n_out], refs[n_out:]
+    sum_ref, outs, x_ref, accs = refs[0], refs[1:n_out], refs[n_out], refs[n_out + 1 :]
     elems, width, sides = pieces[0].shape
     half = width // 2
     me = lax.axis_index("col")
@@ -158,31 +216,39 @@
     group = [me * elems] + [partner(me, k) * elems for k in steps]
     window = [d * elems for d in range(REACH + 1)]
     sources, places = (window, group) if to_group else (group, window)
-    acc_ref[...] = jnp.zeros_like(acc_ref)
+    for acc_ref in accs:
+        acc_ref[...] = jnp.zeros_like(acc_ref)
     for at, ref in zip(sources, pieces):
         x_ref[pl.ds(at, elems)] = ref[...]
 
-    @pl.loop(0, (count_ref[0] + STEP_SLOTS - 1) // STEP_SLOTS)
+    @pl.loop(0, steps_ref[0, 0])
     def _(step):
-        first = step * STEP_SLOTS
+        row, lane = step // (LANES // STEP_SLOTS), step % (LANES // STEP_SLOTS) * STEP_SLOTS
         zero = jnp.zeros((width, sides), x_ref.dtype)
-        for s in range(STEP_SLOTS):
-            tile = tile_ref[pl.ds((first + s) * (half + 1), half), :].astype(x_ref.dtype)
-            x, to = x_ref[from_ref[first + s]], to_ref[first + s]
+        for at in range(0, STEP_SLOTS, SHARE):
+            x = x_ref[key_ref[row, lane + at]]
             w = jnp.concatenate([jnp.concatenate([x, zero], axis=1), jnp.concatenate([zero, x], axis=1)], axis=0)
-            d = jnp.dot(tile, w, preferred_element_type=jnp.float32)
-            acc_ref[to, 0:half, :] += d[:, 0:sides]
-            acc_ref[to, half:width, :] += d[:, sides : 2 * sides]
-
-    total = acc_ref[pl.ds(places[0], elems)]
+            tiles = [tile_ref[pl.ds(slot_ref[row, lane + at + k], half), :] for k in range(SHARE)]
+            d = jnp.dot(
+                jnp.concatenate(tiles, axis=0).astype(x_ref.dtype), w, preferred_element_type=jnp.float32
+            )
+            for k in range(SHARE):
+                to, one, acc_ref = to_ref[row, lane + at + k], slice(k * half, (k + 1) * half), accs[k % CHAINS]
+                acc_ref[to, 0:half, :] += d[one, 0:sides]
+                acc_ref[to, half:width, :] += d[one, sides : 2 * sides]
+
+    def summed(at):
+        return sum(acc_ref[pl.ds(at, elems)] for acc_ref in accs)
+
+    total = summed(places[0])
     for ref in more:
         total = total + ref[...]
     sum_ref[...] = total
     for at, ref in zip(places[1:], outs):
-        put_codes(ref, acc_ref[pl.ds(at, elems)])
-
-
-def products(count, source, target, tiles, pieces, n_out, more=()):
+        put_codes(ref, summed(at))
+
+
+def products(order, tiles, pieces, n_out, more=()):
     elems, width, sides = pieces[0].shape
     n_in, to_group = len(pieces), bool(more)
     code = jax.ShapeDtypeStruct((elems * width + CODE_ROWS, sides), jnp.int16)
@@ -190,16 +256,16 @@
     return pl.pallas_call(
         functools.partial(products_kernel, to_group=to_group, n_in=n_in, n_out=n_out),
         out_shape=[jax.ShapeDtypeStruct((elems, width, sides), jnp.float32)] + [code] * (n_out - 1),
-        in_specs=[scalar] * 3 + [vector] * (1 + n_in + len(more)),
+        in_specs=[scalar] * 4 + [vector] * (1 + n_in + len(more)),
         out_specs=[vector] * n_out,
         scratch_shapes=[
             VMEM((n_in * elems + 1, width, sides), pieces[0].dtype),
-            VMEM((n_out * elems + 1, width, sides), jnp.float32),
-        ],
+        ]
+        + [VMEM((n_out * elems + 1, width, sides), jnp.float32)] * CHAINS,
         compiler_params=pltpu.CompilerParams(vmem_limit_bytes=SUM_MIB * MIB),
         cost_estimate=pl.CostEstimate(flops=1 << 31, bytes_accessed=12 * MIB, transcendentals=0),
         name="row_products" if to_group else "col_products",
-    )(count, source, target, pltpu.with_memory_space_constraint(tiles, VMEM), *pieces, *more)
+    )(*order, pltpu.with_memory_space_constraint(tiles, VMEM), *pieces, *more)
 
 
 def finish_kernel(*refs):
@@ -230,12 +296,12 @@
     reach = range(1, REACH + 1)
     side = [meet(coeffs, "col", k) for k in steps]
     far = [shift(coeffs, "row", -d) for d in reach]
-    tiles, flips, mine, (row, col, land) = make_tiles(blk_count, blk_rows, blk_cols, blocks, coeffs)
-    own, *codes = products(blk_count, row, land, flips, [mine] + side, 1 + len(far))
+    tiles, flips, mine, by_group, by_window = make_tiles(blk_count, blk_rows, blk_cols, blocks, coeffs)
+    own, *codes = products(by_group, flips, [mine] + side, 1 + len(far))
     got = []
     for d, c in zip(reach, codes):
         got.append(shift(c, "row", d))
-    own, *codes = products(blk_count, col, row, tiles, [mine] + far, 1 + len(side), [own])
+    own, *codes = products(by_window, tiles, [mine] + far, 1 + len(side), [own])
     got += [meet(c, "col", k) for k, c in zip(steps, codes)]
     return finish(own, got)
 

time: 46.2 us -> 43.6 us (0.944)
  starting transfers between devices: 17.4 us -> 15.6 us
  waiting for transfers between devices: 14.9 us -> 14.1 us
    ppermute x6, starting transfers between devices: 13.2 us -> 10.3 us  [meet(): lax.ppermute(x, axis, [(i, partner(i, k)) for i in range(lax.axis_size(ax...]
    ppermute x6, waiting for transfers between devices: 10.4 us -> 8.6 us  [shift(): return lax.ppermute(x, axis, [(i, (i + distance) % n) for i in range(n)])]
    ppermute x6, starting transfers between devices: 4.15 us -> 5.32 us  [shift(): return lax.ppermute(x, axis, [(i, (i + distance) % n) for i in range(n)])]
    ppermute x6, waiting for transfers between devices: 4.48 us -> 5.53 us  [meet(): lax.ppermute(x, axis, [(i, partner(i, k)) for i in range(lax.axis_size(ax...]
    pallas_call x2, Pallas kernels: 6.23 us -> 5.5 us  [products(): pl.pallas_call(functools.partial(products_kernel, to_group=to_group, n_in...]
    pallas_call x1, Pallas kernels: 5.8 us -> 6.5 us  [make_tiles(): pl.pallas_call(functools.partial(tiles_kernel, width=width, slots=slots,...]
  transfers between devices with their start and end apart: 12 -> 12, of which waited for: 7 -> 7; matrix products, arithmetic and copies ran while one was open for 0% -> 0% of each run, Pallas kernels for 19% -> 21%
where the time goes in v3:
time: 43.6 us; the launch traced here: 43.4 us
  starting transfers between devices  15.6 us (36%)
  waiting for transfers between devices  14.1 us (32%)
  Pallas kernels  12.9 us (30%)
  between operations  0.73 us (2%)
    ppermute x6, starting transfers between devices, meet(): lax.ppermute(x, axis, [(i, partner(i, k)) for i in range(lax.axis_size(ax...  10.3 us
    ppermute x6, waiting for transfers between devices, shift(): return lax.ppermute(x, axis, [(i, (i + distance) % n) for i in range(n)])  8.6 us
    pallas_call x1, Pallas kernels, make_tiles(): pl.pallas_call(functools.partial(tiles_kernel, width=width, slots=slots,...  6.5 us
    ppermute x6, waiting for transfers between devices, meet(): lax.ppermute(x, axis, [(i, partner(i, k)) for i in range(lax.axis_size(ax...  5.53 us
    pallas_call x2, Pallas kernels, products(): pl.pallas_call(functools.partial(products_kernel, to_group=to_group, n_in...  5.5 us
    ppermute x6, starting transfers between devices, shift(): return lax.ppermute(x, axis, [(i, (i + distance) % n) for i in range(n)])  5.32 us
    pallas_call x1, Pallas kernels, finish(): pl.pallas_call(finish_kernel, out_shape=jax.ShapeDtypeStruct(own.shape, j...  0.94 us
  transfers between devices with their start and end apart: 12, of which 7 were waited for; matrix products, arithmetic and copies ran while one was open for 0% of the time, Pallas kernels for 21%

profile of v3, /device:TPU:0, one launch (start us, length us, event | category | flops | bytes accessed | tf_op | source)
XLA Modules:
  0.0 43.4 jit_solution(15268786554681050074)
XLA Ops:
  0.0 3.0 %collective-permute-start.3 = (bf16[8,64,128]{2,1,0:T(8,128)(2,1)}, bf16[8,64,128]{2,1,0:T(8,128)(2,1)S(1)}, u32[]{:S(2)}, u32[]{:S(2)}) collective-permute-start(bf16[8,64,128]{2,1,0:T(8,128)(2,1)} %own_hbm.1), channel_id=1, source_target_pairs={{0,1},{1,0},{2,3},{3,2},{4,5},{5,4},{6,7},{7,6},{8,9},{9,8},{10,11... | collective-permute-start | bytes 393224 | tf_op jit(solution)/shard_map/ppermute | solution.py:33
  3.0 1.5 %collective-permute-start.4 = (bf16[8,64,128]{2,1,0:T(8,128)(2,1)}, bf16[8,64,128]{2,1,0:T(8,128)(2,1)S(1)}, u32[]{:S(2)}, u32[]{:S(2)}) collective-permute-start(bf16[8,64,128]{2,1,0:T(8,128)(2,1)} %own_hbm.1), channel_id=1, source_target_pairs={{0,2},{1,3},{2,0},{3,1},{4,6},{5,7},{6,4},{7,5},{8,10},{9,11},{10,... | collective-permute-start | bytes 393224 | tf_op jit(solution)/shard_map/ppermute | solution.py:33
  4.5 0.0 collective-permute-start.5
  4.5 2.7 %collective-permute-start = (bf16[8,64,128]{2,1,0:T(8,128)(2,1)}, bf16[8,64,128]{2,1,0:T(8,128)(2,1)S(1)}, u32[]{:S(2)}, u32[]{:S(2)}) collective-permute-start(bf16[8,64,128]{2,1,0:T(8,128)(2,1)} %own_hbm.1), channel_id=1, source_target_pairs={{0,28},{4,0},{8,4},{12,8},{16,12},{20,16},{24,20},{28,24},{1,29},{... | collective-permute-start | bytes 393224 | tf_op jit(solution)/shard_map/ppermute | solution.py:38
  7.2 1.4 %collective-permute-start.1 = (bf16[8,64,128]{2,1,0:T(8,128)(2,1)}, bf16[8,64,128]{2,1,0:T(8,128)(2,1)S(1)}, u32[]{:S(2)}, u32[]{:S(2)}) collective-permute-start(bf16[8,64,128]{2,1,0:T(8,128)(2,1)} %own_hbm.1), channel_id=1, source_target_pairs={{0,24},{4,28},{8,0},{12,4},{16,8},{20,12},{24,16},{28,20},{1,25},{... | collective-permute-start | bytes 393224 | tf_op jit(solution)/shard_map/ppermute | solution.py:38
  9.2 6.5 %tiles.1 = (f32[16896,128]{1,0:T(8,128)S(1)}, f32[16896,128]{1,0:T(8,128)S(1)}, bf16[8,64,128]{2,1,0:T(8,128)(2,1)S(1)}, s32[5,128]{1,0:T(8,128)S(1)}, s32[5,128...) custom-call(s32[1]{0:T(128)S(6)} %copy.6.count_ref, ...), custom_call_target="tpu_custom_call" | custom-call | flops 1073741824 | bytes 25165824 | tf_op jit(solution)/shard_map/tiles/pallas_call | solution.py:172
  15.7 0.0 collective-permute-done.3.refs_1_
  15.7 0.1 collective-permute-start.2
  15.8 0.0 collective-permute-done.4.refs_2_
  15.8 0.0 collective-permute-done.5.refs_3_
  15.8 2.7 %col_products.1 = (f32[8,64,128]{2,1,0:T(8,128)S(1)}, s16[528,128]{1,0:T(8,128)(2,1)S(1)}, s16[528,128]{1,0:T(8,128)(2,1)S(1)}, s16[528,128]{1,0:T(8,128)(2,1)S(1)}) custom-call(s32[5,128]{1,0:T(8,128)S(1)} %get-tuple-element.30.slot_ref, s32[5,128]{1,0:T(8,128)S(1)} %get-tuple-element.31.key_ref, s32[5,128]{1,0:T(8,128)S(1)} %get-tuple-element.32.to_ref, ...), custom_call_target="tpu_custom_call" | custom-call | flops 2147483648 | bytes 12582912 | tf_op jit(solution)/shard_map/col_products/pallas_call | solution.py:256
  18.6 0.0 collective-permute-done.refs_1_
  18.6 0.0 collective-permute-done.1.refs_2_
  18.6 1.8 %collective-permute-done.2.refs_3_ = bf16[8,64,128]{2,1,0:T(8,128)(2,1)S(1)} collective-permute-done((bf16[8,64,128]{2,1,0:T(8,128)(2,1)}, bf16[8,64,128]{2,1,0:T(8,128)(2,1)S(1)}, u32[]{:S(2)}, u32[]{:S(2)}) %collective-permute-start.2) | collective-permute-done | bytes 131104 | tf_op jit(solution)/shard_map/ppermute | solution.py:38
  20.4 2.8 %row_products.1 = (f32[8,64,128]{2,1,0:T(8,128)S(1)}, s16[528,128]{1,0:T(8,128)(2,1)S(1)}, s16[528,128]{1,0:T(8,128)(2,1)S(1)}, s16[528,128]{1,0:T(8,128)(2,1)S(1)}) custom-call(s32[5,128]{1,0:T(8,128)S(1)} %get-tuple-element.24.slot_ref, s32[5,128]{1,0:T(8,128)S(1)} %get-tuple-element.25.key_ref, s32[5,128]{1,0:T(8,128)S(1)} %get-tuple-element.26.to_ref, ...), custom_call_target="tpu_custom_call" | custom-call | flops 2147483648 | bytes 12582912 | tf_op jit(solution)/shard_map/row_products/pallas_call | solution.py:256
  23.2 4.2 %collective-permute-start.10 = (s16[528,128]{1,0:T(8,128)(2,1)S(1)}, s16[528,128]{1,0:T(8,128)(2,1)S(1)}, u32[]{:S(2)}, u32[]{:S(2)}) collective-permute-start(s16[528,128]{1,0:T(8,128)(2,1)S(1)} %get-tuple-element.41), channel_id=1, source_target_pairs={{0,2},{1,3},{2,0},{3,1},{4,6},{5,7},{6,4},{7,5},{8,10},{9,11},{10,... | collective-permute-start | bytes 405512 | tf_op jit(solution)/shard_map/ppermute | solution.py:33
  27.4 0.0 collective-permute-start.11
  27.4 1.5 %collective-permute-start.9 = (s16[528,128]{1,0:T(8,128)(2,1)S(1)}, s16[528,128]{1,0:T(8,128)(2,1)S(1)}, u32[]{:S(2)}, u32[]{:S(2)}) collective-permute-start(s16[528,128]{1,0:T(8,128)(2,1)S(1)} %get-tuple-element.40), channel_id=1, source_target_pairs={{0,1},{1,0},{2,3},{3,2},{4,5},{5,4},{6,7},{7,6},{8,9},{9,8},{10,11... | collective-permute-start | bytes 405512 | tf_op jit(solution)/shard_map/ppermute | solution.py:33
  29.0 0.0 collective-permute-start.6
  29.0 1.2 %collective-permute-start.7 = (s16[528,128]{1,0:T(8,128)(2,1)S(1)}, s16[528,128]{1,0:T(8,128)(2,1)S(1)}, u32[]{:S(2)}, u32[]{:S(2)}) collective-permute-start(s16[528,128]{1,0:T(8,128)(2,1)S(1)} %get-tuple-element.38), channel_id=1, source_target_pairs={{0,8},{4,12},{8,16},{12,20},{16,24},{20,28},{24,0},{28,4},{1,9},{5... | collective-permute-start | bytes 405512 | tf_op jit(solution)/shard_map/ppermute | solution.py:38
  30.2 3.8 %collective-permute-done.10.refs_5_ = s16[528,128]{1,0:T(8,128)(2,1)S(1)} collective-permute-done((s16[528,128]{1,0:T(8,128)(2,1)S(1)}, s16[528,128]{1,0:T(8,128)(2,1)S(1)}, u32[]{:S(2)}, u32[]{:S(2)}) %collective-permute-start.10) | collective-permute-done | bytes 135200 | tf_op jit(solution)/shard_map/ppermute | solution.py:33
  33.9 0.0 collective-permute-start.8
  33.9 0.9 %collective-permute-done.11.refs_6_ = s16[528,128]{1,0:T(8,128)(2,1)S(1)} collective-permute-done((s16[528,128]{1,0:T(8,128)(2,1)S(1)}, s16[528,128]{1,0:T(8,128)(2,1)S(1)}, u32[]{:S(2)}, u32[]{:S(2)}) %collective-permute-start.11) | collective-permute-done | bytes 135200 | tf_op jit(solution)/shard_map/ppermute | solution.py:33
  34.8 0.8 %collective-permute-done.9.refs_4_ = s16[528,128]{1,0:T(8,128)(2,1)S(1)} collective-permute-done((s16[528,128]{1,0:T(8,128)(2,1)S(1)}, s16[528,128]{1,0:T(8,128)(2,1)S(1)}, u32[]{:S(2)}, u32[]{:S(2)}) %collective-permute-start.9) | collective-permute-done | bytes 135200 | tf_op jit(solution)/shard_map/ppermute | solution.py:33
  35.7 0.4 collective-permute-done.6.refs_1_
  36.1 1.2 %collective-permute-done.7.refs_2_ = s16[528,128]{1,0:T(8,128)(2,1)S(1)} collective-permute-done((s16[528,128]{1,0:T(8,128)(2,1)S(1)}, s16[528,128]{1,0:T(8,128)(2,1)S(1)}, u32[]{:S(2)}, u32[]{:S(2)}) %collective-permute-start.7) | collective-permute-done | bytes 135200 | tf_op jit(solution)/shard_map/ppermute | solution.py:38
  37.2 5.2 %collective-permute-done.8.refs_3_ = s16[528,128]{1,0:T(8,128)(2,1)S(1)} collective-permute-done((s16[528,128]{1,0:T(8,128)(2,1)S(1)}, s16[528,128]{1,0:T(8,128)(2,1)S(1)}, u32[]{:S(2)}, u32[]{:S(2)}) %collective-permute-start.8) | collective-permute-done | bytes 135200 | tf_op jit(solution)/shard_map/ppermute | solution.py:38
  42.5 0.9 %finish.1 = f32[8,64,128]{2,1,0:T(8,128)} custom-call(f32[8,64,128]{2,1,0:T(8,128)S(1)} %get-tuple-element.36.refs_0_, s16[528,128]{1,0:T(8,128)(2,1)S(1)} %collective-permute-done.6.refs_1_, s16[528,128]{1,0:T(8,128)(2,1)S(1)} %collective-permute-done.7.refs_2_, s16[528,128]{1,0:T(8,128)(2,1)S(1)} %collective-permute-done.8.refs_3_, ...), custom_call_target="tpu_custom_call" | custom-call | tf_op jit(solution)/shard_map/finish/pallas_call | solution.py:284
Async XLA Ops:
  0.0 15.7 %collective-permute-start.3 = (bf16[8,64,128]{2,1,0:T(8,128)(2,1)}, bf16[8,64,128]{2,1,0:T(8,128)(2,1)S(1)}, u32[]{:S(2)}, u32[]{:S(2)}) collective-permute-start(bf16[8,64,128]{2,1,0:T(8,128)(2,1)} %own_hbm.1), channel_id=1, source_target_pairs={{0,1},{1,0},{2,3},{3,2},{4,5},{5,4},{6,7},{7,6},{8,9},{9,8},{10,11... | collective-permute-start | bytes 393224 | tf_op jit(solution)/shard_map/ppermute | solution.py:33
  3.0 12.8 %collective-permute-start.4 = (bf16[8,64,128]{2,1,0:T(8,128)(2,1)}, bf16[8,64,128]{2,1,0:T(8,128)(2,1)S(1)}, u32[]{:S(2)}, u32[]{:S(2)}) collective-permute-start(bf16[8,64,128]{2,1,0:T(8,128)(2,1)} %own_hbm.1), channel_id=1, source_target_pairs={{0,2},{1,3},{2,0},{3,1},{4,6},{5,7},{6,4},{7,5},{8,10},{9,11},{10,... | collective-permute-start | bytes 393224 | tf_op jit(solution)/shard_map/ppermute | solution.py:33
  4.5 11.3 %collective-permute-start.5 = (bf16[8,64,128]{2,1,0:T(8,128)(2,1)}, bf16[8,64,128]{2,1,0:T(8,128)(2,1)S(1)}, u32[]{:S(2)}, u32[]{:S(2)}) collective-permute-start(bf16[8,64,128]{2,1,0:T(8,128)(2,1)} %own_hbm.1), channel_id=1, source_target_pairs={{0,3},{1,2},{2,1},{3,0},{4,7},{5,6},{6,5},{7,4},{8,11},{9,10},{10,... | collective-permute-start | bytes 393224 | tf_op jit(solution)/shard_map/ppermute | solution.py:33
  4.5 14.1 %collective-permute-start = (bf16[8,64,128]{2,1,0:T(8,128)(2,1)}, bf16[8,64,128]{2,1,0:T(8,128)(2,1)S(1)}, u32[]{:S(2)}, u32[]{:S(2)}) collective-permute-start(bf16[8,64,128]{2,1,0:T(8,128)(2,1)} %own_hbm.1), channel_id=1, source_target_pairs={{0,28},{4,0},{8,4},{12,8},{16,12},{20,16},{24,20},{28,24},{1,29},{... | collective-permute-start | bytes 393224 | tf_op jit(solution)/shard_map/ppermute | solution.py:38
  7.2 11.4 %collective-permute-start.1 = (bf16[8,64,128]{2,1,0:T(8,128)(2,1)}, bf16[8,64,128]{2,1,0:T(8,128)(2,1)S(1)}, u32[]{:S(2)}, u32[]{:S(2)}) collective-permute-start(bf16[8,64,128]{2,1,0:T(8,128)(2,1)} %own_hbm.1), channel_id=1, source_target_pairs={{0,24},{4,28},{8,0},{12,4},{16,8},{20,12},{24,16},{28,20},{1,25},{... | collective-permute-start | bytes 393224 | tf_op jit(solution)/shard_map/ppermute | solution.py:38
  15.7 4.7 %collective-permute-start.2 = (bf16[8,64,128]{2,1,0:T(8,128)(2,1)}, bf16[8,64,128]{2,1,0:T(8,128)(2,1)S(1)}, u32[]{:S(2)}, u32[]{:S(2)}) collective-permute-start(bf16[8,64,128]{2,1,0:T(8,128)(2,1)} %own_hbm.1), channel_id=1, source_target_pairs={{0,20},{4,24},{8,28},{12,0},{16,4},{20,8},{24,12},{28,16},{1,21},{... | collective-permute-start | bytes 393224 | tf_op jit(solution)/shard_map/ppermute | solution.py:38
  23.2 10.7 %collective-permute-start.10 = (s16[528,128]{1,0:T(8,128)(2,1)S(1)}, s16[528,128]{1,0:T(8,128)(2,1)S(1)}, u32[]{:S(2)}, u32[]{:S(2)}) collective-permute-start(s16[528,128]{1,0:T(8,128)(2,1)S(1)} %get-tuple-element.41), channel_id=1, source_target_pairs={{0,2},{1,3},{2,0},{3,1},{4,6},{5,7},{6,4},{7,5},{8,10},{9,11},{10,... | collective-permute-start | bytes 405512 | tf_op jit(solution)/shard_map/ppermute | solution.py:33
  27.4 7.4 %collective-permute-start.11 = (s16[528,128]{1,0:T(8,128)(2,1)S(1)}, s16[528,128]{1,0:T(8,128)(2,1)S(1)}, u32[]{:S(2)}, u32[]{:S(2)}) collective-permute-start(s16[528,128]{1,0:T(8,128)(2,1)S(1)} %get-tuple-element.42), channel_id=1, source_target_pairs={{0,3},{1,2},{2,1},{3,0},{4,7},{5,6},{6,5},{7,4},{8,11},{9,10},{10,... | collective-permute-start | bytes 405512 | tf_op jit(solution)/shard_map/ppermute | solution.py:33
  27.4 8.2 %collective-permute-start.9 = (s16[528,128]{1,0:T(8,128)(2,1)S(1)}, s16[528,128]{1,0:T(8,128)(2,1)S(1)}, u32[]{:S(2)}, u32[]{:S(2)}) collective-permute-start(s16[528,128]{1,0:T(8,128)(2,1)S(1)} %get-tuple-element.40), channel_id=1, source_target_pairs={{0,1},{1,0},{2,3},{3,2},{4,5},{5,4},{6,7},{7,6},{8,9},{9,8},{10,11... | collective-permute-start | bytes 405512 | tf_op jit(solution)/shard_map/ppermute | solution.py:33
  29.0 7.1 %collective-permute-start.6 = (s16[528,128]{1,0:T(8,128)(2,1)S(1)}, s16[528,128]{1,0:T(8,128)(2,1)S(1)}, u32[]{:S(2)}, u32[]{:S(2)}) collective-permute-start(s16[528,128]{1,0:T(8,128)(2,1)S(1)} %get-tuple-element.37), channel_id=1, source_target_pairs={{0,4},{4,8},{8,12},{12,16},{16,20},{20,24},{24,28},{28,0},{1,5},{5... | collective-permute-start | bytes 405512 | tf_op jit(solution)/shard_map/ppermute | solution.py:38
  29.0 8.3 %collective-permute-start.7 = (s16[528,128]{1,0:T(8,128)(2,1)S(1)}, s16[528,128]{1,0:T(8,128)(2,1)S(1)}, u32[]{:S(2)}, u32[]{:S(2)}) collective-permute-start(s16[528,128]{1,0:T(8,128)(2,1)S(1)} %get-tuple-element.38), channel_id=1, source_target_pairs={{0,8},{4,12},{8,16},{12,20},{16,24},{20,28},{24,0},{28,4},{1,9},{5... | collective-permute-start | bytes 405512 | tf_op jit(solution)/shard_map/ppermute | solution.py:38
  33.9 8.5 %collective-permute-start.8 = (s16[528,128]{1,0:T(8,128)(2,1)S(1)}, s16[528,128]{1,0:T(8,128)(2,1)S(1)}, u32[]{:S(2)}, u32[]{:S(2)}) collective-permute-start(s16[528,128]{1,0:T(8,128)(2,1)S(1)} %get-tuple-element.39), channel_id=1, source_target_pairs={{0,12},{4,16},{8,20},{12,24},{16,28},{20,0},{24,4},{28,8},{1,13},{... | collective-permute-start | bytes 405512 | tf_op jit(solution)/shard_map/ppermute | solution.py:38
